TPU v7x, 128 devices: a whole 4x4x4 slice. The times are simulated.
128 devices in a mesh: cluster: 8 (over z, core), seq: 16 (over x, y).
Axes of the slice: x: 4, y: 4, z: 4, core: 2. Of those that a mesh axis runs over, the one named last changes fastest.
Arguments:
- nodes: bfloat16 [65536, 1024], P(('cluster', 'seq')), may hold values from -48 to 48
- w_qkv: bfloat16 [1024, 3072], replicated, may hold values from -0.1875 to 0.1875
- w_out: bfloat16 [1024, 1024], replicated, may hold values from -1.5 to 1.5
- kv_ids: int32 [512, 16], P('cluster'), may hold values from 0 to 511, as said below
- counts: int32 [512], P('cluster'), may hold values from 13 to 16, as said below
Outputs:
- attended_out: bfloat16 [65536, 1024], P(('cluster', 'seq'))
Inputs may be any that keep to these rules, and one draw needn't show every extreme that they name: `kv_ids`: entries name blocks; the cluster of block b is b // 64. For query block q, entry 0 is q itself, entries 0 to 11 are distinct blocks of q's cluster, and the last 4 entries are distinct blocks of other clusters. Over all entries of the query blocks of one cluster, at most 16 distinct blocks of any one other cluster are named, and exactly 16 for some pair of clusters. The first counts[q] entries of query block q's list are valid, the others are padding.
All inputs are finite; a program needn't handle non-finite values.
Results may differ from a plain program's by a relative error of at most 0.012.
Values may be sent and summed in bfloat16 or wider, within the bound.
A program may use at most 128 MiB of HBM per device.

v0:
```python
import jax
import jax.numpy as jnp
from jax import lax
from jax.sharding import PartitionSpec as P

D = 1024
HEADS = 16
HD = 64
BLK = 128
KVB = 16
REMOTE = 4


def on_device(nodes, w_qkv, w_out, kv_ids, counts):
    seq_size = lax.axis_size("seq")
    node_rows = nodes.shape[0]
    heads_dev = HEADS // seq_size
    w_grouped = w_qkv.reshape(D, seq_size, heads_dev, 3, HD)
    w_query = w_grouped[:, :, :, 0].reshape(D, seq_size, heads_dev * HD)
    w_keyval = w_grouped[:, :, :, 1:].reshape(D, seq_size, heads_dev * 2 * HD)
    query_proj = jnp.einsum(
        "rd,dsf->srf", nodes, w_query, preferred_element_type=jnp.float32
    ).astype(jnp.bfloat16)
    keyval_proj = jnp.einsum(
        "rd,dsf->srf", nodes, w_keyval, preferred_element_type=jnp.float32
    ).astype(jnp.bfloat16)
    query_recv, keyval_recv = (
        lax.all_to_all(query_proj, "seq", split_axis=0, concat_axis=0, tiled=True),
        lax.all_to_all(keyval_proj, "seq", split_axis=0, concat_axis=0, tiled=True),
    )
    cluster_rows = seq_size * node_rows
    block_count = cluster_rows // BLK
    queries = query_recv.reshape(block_count, BLK, heads_dev, HD)
    keyval_blocks = keyval_recv.reshape(block_count, BLK, heads_dev, 2, HD)
    key_table = jnp.transpose(keyval_blocks[:, :, :, 0], (0, 2, 3, 1))
    value_table = jnp.transpose(keyval_blocks[:, :, :, 1], (0, 2, 1, 3))
    cluster = lax.axis_index("cluster")
    local_ids = kv_ids[:, : KVB - REMOTE] - cluster * block_count
    remote_ids = kv_ids[:, KVB - REMOTE :]
    slot_ids = jnp.arange(KVB, dtype=jnp.int32)
    is_valid = slot_ids[None, :] < counts[:, None]
    far_keys, far_values = (
        lax.all_gather(key_table, "cluster", axis=0, tiled=True),
        lax.all_gather(value_table, "cluster", axis=0, tiled=True),
    )
    groups = block_count // 4
    scale = HD ** (-0.5)

    def attend(packed):
        query_blk, near_ids, far_ids, valid_blk = packed
        near_k = key_table[near_ids]
        far_k = far_keys[far_ids]
        near_v = value_table[near_ids]
        far_v = far_values[far_ids]
        near_scores = (
            jnp.einsum("qahe,qjhek->qhajk", query_blk, near_k, preferred_element_type=jnp.float32)
            * scale
        )
        far_scores = (
            jnp.einsum("qahe,qjhek->qhajk", query_blk, far_k, preferred_element_type=jnp.float32)
            * scale
        )
        near_scores = jnp.where(valid_blk[:, None, None, : KVB - REMOTE, None], near_scores, -1e30)
        far_scores = jnp.where(valid_blk[:, None, None, KVB - REMOTE :, None], far_scores, -1e30)
        row_top = jnp.maximum(
            jnp.max(near_scores, axis=(3, 4), keepdims=True),
            jnp.max(far_scores, axis=(3, 4), keepdims=True),
        )
        near_exp = jnp.exp(near_scores - row_top)
        far_exp = jnp.exp(far_scores - row_top)
        row_total = jnp.sum(near_exp, axis=(3, 4), keepdims=True) + jnp.sum(
            far_exp, axis=(3, 4), keepdims=True
        )
        near_weight = (near_exp / row_total).astype(jnp.bfloat16)
        far_weight = (far_exp / row_total).astype(jnp.bfloat16)
        summed = jnp.einsum(
            "qhajk,qjhke->qahe", near_weight, near_v, preferred_element_type=jnp.float32
        )
        summed = summed + jnp.einsum(
            "qhajk,qjhke->qahe", far_weight, far_v, preferred_element_type=jnp.float32
        )
        return summed.astype(jnp.bfloat16)

    attended = lax.map(
        attend,
        (
            queries.reshape(groups, 4, BLK, heads_dev, HD),
            local_ids.reshape(groups, 4, KVB - REMOTE),
            remote_ids.reshape(groups, 4, REMOTE),
            is_valid.reshape(groups, 4, KVB),
        ),
    )
    attended = attended.reshape(seq_size, node_rows, heads_dev * HD)
    returned = lax.all_to_all(attended, "seq", split_axis=0, concat_axis=0, tiled=True)
    w_split = w_out.reshape(seq_size, heads_dev * HD, D)
    return jnp.einsum("srf,sfd->rd", returned, w_split, preferred_element_type=jnp.float32).astype(
        jnp.bfloat16
    )


def solution(mesh):
    placed = (P(("cluster", "seq"), None), P(), P(), P("cluster", None), P("cluster"))
    return jax.shard_map(
        on_device,
        mesh=mesh,
        in_specs=placed,
        out_specs=P(("cluster", "seq"), None),
        check_vma=False,
    )
```

profile of v0, /device:TPU:1, one launch (start us, length us, event | category | flops | bytes accessed | tf_op | source)
XLA Modules:
  0.0 599.8 jit_solution(15980403184799001119)
XLA Ops:
  6.5 8.8 %copy.22 = bf16[1024,3072]{0,1:T(8,128)(2,1)} copy(bf16[1024,3072]{1,0:T(8,128)(2,1)} %param.8) | data formatting | bytes 12582912 | tf_op args[1]
  20.5 33.9 %all_to_all.15 = bf16[16,512,128]{1,2,0:T(8,128)(2,1)S(1)} all-to-all(bf16[16,512,128]{1,2,0:T(8,128)(2,1)S(1)} %convert_bitcast_fusion), channel_id=1, replica_groups=mesh['cluster'=8,'seq'=16] {'seq'}, dimensions={0} | all-to-all | bytes 4194304 | tf_op jit(solution)/shard_map/all_to_all | solution.py:29
  56.9 4.4 reshape.168
  61.3 4.0 fusion.18
  70.1 4.5 all-to-all-start.1
  75.6 13.8 %all-to-all-done.1 = bf16[16,512,64]{1,2,0:T(8,128)(2,1)S(1)} async-done(((bf16[16,512,64]{1,2,0:T(8,128)(2,1)}), bf16[16,512,64]{1,2,0:T(8,128)(2,1)S(1)}, u32[]{:S(2)}, u32[]{:S(2)}) %all-to-all-start.1) | async-done | bytes 1048608 | tf_op jit(solution)/shard_map/all_to_all | solution.py:28
  95.7 21.4 %all-gather.6.cloned.1.call-done = bf16[512,128,1,1,64]{1,0,4,3,2:T(8,128)(2,1)} async-done(((bf16[64,128,1,1,64]{1,0,4,3,2:T(8,128)(2,1)}), bf16[512,128,1,1,64]{1,0,4,3,2:T(8,128)(2,1)}) %all-gather.6.cloned.1.call-update) | async-done | bytes 8388624 | tf_op jit(solution)/shard_map/all_gather | solution.py:44
  117.1 17.9 %copy.30 = bf16[512,1,128,64]{3,2,1,0:T(8,128)(2,1)} copy(bf16[512,1,128,64]{2,0,3,1:T(8,128)(2,1)} %bitcast.149) | data formatting | bytes 16777216 | tf_op jit(solution)/shard_map/while | solution.py:84
  135.0 33.7 %all-gather.4.cloned.1.call-done = bf16[512,1,64,128]{3,0,2,1:T(8,128)(2,1)} async-done(((bf16[64,1,64,128]{3,0,2,1:T(8,128)(2,1)}), bf16[512,1,64,128]{3,0,2,1:T(8,128)(2,1)}) %all-gather.4.cloned.1.call-update) | async-done | bytes 8388624 | tf_op jit(solution)/shard_map/all_gather | solution.py:43
  168.8 12.0 %copy.29 = bf16[512,1,64,128]{3,2,1,0:T(8,128)(2,1)} copy(bf16[512,1,64,128]{3,0,2,1:T(8,128)(2,1)} %all-gather.4.cloned.1.call-done) | data formatting | bytes 16777216 | tf_op jit(solution)/shard_map/while | solution.py:84
  180.8 386.2 %while.10 = (s32[]{:T(128)}, bf16[16,4,128,1,64]{2,1,4,0,3:T(4,128)(2,1)}, s32[16,4,12]{2,1,0:T(4,128)S(1)}, bf16[64,1,128,64]{3,2,1,0:T(8,128)(2,1)}, pred[16,4...) while((s32[]{:T(128)}, ...), condition=%wide.region_5.6_spmd, body=%wide.region_0.5_spmd.sunk | while | flops 280036544 | bytes 32221496 | solution.py:84
  182.6 4.0 gather_fusion.1
  186.6 7.2 %gather_fusion = bf16[16,128,64]{2,1,0:T(8,128)(2,1)} fusion(bf16[512,128,64]{2,1,0:T(8,128)(2,1)} %bitcast.144, s32[1024]{0:T(1024)S(1)} %pad_clamp_fusion.4), kind=kCustom, calls=%fused_computation.3.clone.1 | custom fusion | bytes 524352 | tf_op jit(solution)/shard_map/while/body/eval_jaxpr/gather | solution.py:54
  206.7 4.0 gather_fusion.1
  210.7 7.2 %gather_fusion = bf16[16,128,64]{2,1,0:T(8,128)(2,1)} fusion(bf16[512,128,64]{2,1,0:T(8,128)(2,1)} %bitcast.144, s32[1024]{0:T(1024)S(1)} %pad_clamp_fusion.4), kind=kCustom, calls=%fused_computation.3.clone.1 | custom fusion | bytes 524352 | tf_op jit(solution)/shard_map/while/body/eval_jaxpr/gather | solution.py:54
  230.9 4.0 gather_fusion.1
  234.9 7.2 %gather_fusion = bf16[16,128,64]{2,1,0:T(8,128)(2,1)} fusion(bf16[512,128,64]{2,1,0:T(8,128)(2,1)} %bitcast.144, s32[1024]{0:T(1024)S(1)} %pad_clamp_fusion.4), kind=kCustom, calls=%fused_computation.3.clone.1 | custom fusion | bytes 524352 | tf_op jit(solution)/shard_map/while/body/eval_jaxpr/gather | solution.py:54
  255.1 4.0 gather_fusion.1
  259.1 7.2 %gather_fusion = bf16[16,128,64]{2,1,0:T(8,128)(2,1)} fusion(bf16[512,128,64]{2,1,0:T(8,128)(2,1)} %bitcast.144, s32[1024]{0:T(1024)S(1)} %pad_clamp_fusion.4), kind=kCustom, calls=%fused_computation.3.clone.1 | custom fusion | bytes 524352 | tf_op jit(solution)/shard_map/while/body/eval_jaxpr/gather | solution.py:54
  283.2 7.2 %gather_fusion = bf16[16,128,64]{2,1,0:T(8,128)(2,1)} fusion(bf16[512,128,64]{2,1,0:T(8,128)(2,1)} %bitcast.144, s32[1024]{0:T(1024)S(1)} %pad_clamp_fusion.4), kind=kCustom, calls=%fused_computation.3.clone.1 | custom fusion | bytes 524352 | tf_op jit(solution)/shard_map/while/body/eval_jaxpr/gather | solution.py:54
  307.3 7.2 %gather_fusion = bf16[16,128,64]{2,1,0:T(8,128)(2,1)} fusion(bf16[512,128,64]{2,1,0:T(8,128)(2,1)} %bitcast.144, s32[1024]{0:T(1024)S(1)} %pad_clamp_fusion.4), kind=kCustom, calls=%fused_computation.3.clone.1 | custom fusion | bytes 524352 | tf_op jit(solution)/shard_map/while/body/eval_jaxpr/gather | solution.py:54
  331.4 7.2 %gather_fusion = bf16[16,128,64]{2,1,0:T(8,128)(2,1)} fusion(bf16[512,128,64]{2,1,0:T(8,128)(2,1)} %bitcast.144, s32[1024]{0:T(1024)S(1)} %pad_clamp_fusion.4), kind=kCustom, calls=%fused_computation.3.clone.1 | custom fusion | bytes 524352 | tf_op jit(solution)/shard_map/while/body/eval_jaxpr/gather | solution.py:54
  355.5 7.2 %gather_fusion = bf16[16,128,64]{2,1,0:T(8,128)(2,1)} fusion(bf16[512,128,64]{2,1,0:T(8,128)(2,1)} %bitcast.144, s32[1024]{0:T(1024)S(1)} %pad_clamp_fusion.4), kind=kCustom, calls=%fused_computation.3.clone.1 | custom fusion | bytes 524352 | tf_op jit(solution)/shard_map/while/body/eval_jaxpr/gather | solution.py:54
  379.6 7.2 %gather_fusion = bf16[16,128,64]{2,1,0:T(8,128)(2,1)} fusion(bf16[512,128,64]{2,1,0:T(8,128)(2,1)} %bitcast.144, s32[1024]{0:T(1024)S(1)} %pad_clamp_fusion.4), kind=kCustom, calls=%fused_computation.3.clone.1 | custom fusion | bytes 524352 | tf_op jit(solution)/shard_map/while/body/eval_jaxpr/gather | solution.py:54
  403.8 7.2 %gather_fusion = bf16[16,128,64]{2,1,0:T(8,128)(2,1)} fusion(bf16[512,128,64]{2,1,0:T(8,128)(2,1)} %bitcast.144, s32[1024]{0:T(1024)S(1)} %pad_clamp_fusion.4), kind=kCustom, calls=%fused_computation.3.clone.1 | custom fusion | bytes 524352 | tf_op jit(solution)/shard_map/while/body/eval_jaxpr/gather | solution.py:54
  428.0 7.2 %gather_fusion = bf16[16,128,64]{2,1,0:T(8,128)(2,1)} fusion(bf16[512,128,64]{2,1,0:T(8,128)(2,1)} %bitcast.144, s32[1024]{0:T(1024)S(1)} %pad_clamp_fusion.4), kind=kCustom, calls=%fused_computation.3.clone.1 | custom fusion | bytes 524352 | tf_op jit(solution)/shard_map/while/body/eval_jaxpr/gather | solution.py:54
  452.2 7.2 %gather_fusion = bf16[16,128,64]{2,1,0:T(8,128)(2,1)} fusion(bf16[512,128,64]{2,1,0:T(8,128)(2,1)} %bitcast.144, s32[1024]{0:T(1024)S(1)} %pad_clamp_fusion.4), kind=kCustom, calls=%fused_computation.3.clone.1 | custom fusion | bytes 524352 | tf_op jit(solution)/shard_map/while/body/eval_jaxpr/gather | solution.py:54
  476.2 7.2 %gather_fusion = bf16[16,128,64]{2,1,0:T(8,128)(2,1)} fusion(bf16[512,128,64]{2,1,0:T(8,128)(2,1)} %bitcast.144, s32[1024]{0:T(1024)S(1)} %pad_clamp_fusion.4), kind=kCustom, calls=%fused_computation.3.clone.1 | custom fusion | bytes 524352 | tf_op jit(solution)/shard_map/while/body/eval_jaxpr/gather | solution.py:54
  500.4 7.2 %gather_fusion = bf16[16,128,64]{2,1,0:T(8,128)(2,1)} fusion(bf16[512,128,64]{2,1,0:T(8,128)(2,1)} %bitcast.144, s32[1024]{0:T(1024)S(1)} %pad_clamp_fusion.4), kind=kCustom, calls=%fused_computation.3.clone.1 | custom fusion | bytes 524352 | tf_op jit(solution)/shard_map/while/body/eval_jaxpr/gather | solution.py:54
  524.5 7.2 %gather_fusion = bf16[16,128,64]{2,1,0:T(8,128)(2,1)} fusion(bf16[512,128,64]{2,1,0:T(8,128)(2,1)} %bitcast.144, s32[1024]{0:T(1024)S(1)} %pad_clamp_fusion.4), kind=kCustom, calls=%fused_computation.3.clone.1 | custom fusion | bytes 524352 | tf_op jit(solution)/shard_map/while/body/eval_jaxpr/gather | solution.py:54
  548.6 7.2 %gather_fusion = bf16[16,128,64]{2,1,0:T(8,128)(2,1)} fusion(bf16[512,128,64]{2,1,0:T(8,128)(2,1)} %bitcast.144, s32[1024]{0:T(1024)S(1)} %pad_clamp_fusion.4), kind=kCustom, calls=%fused_computation.3.clone.1 | custom fusion | bytes 524352 | tf_op jit(solution)/shard_map/while/body/eval_jaxpr/gather | solution.py:54
  568.5 22.3 %all_to_all.16 = bf16[16,512,64]{1,2,0:T(8,128)(2,1)S(1)} all-to-all(bf16[16,512,64]{1,2,0:T(8,128)(2,1)S(1)} %reshape.170), channel_id=1, replica_groups=mesh['cluster'=8,'seq'=16] {'seq'}, dimensions={0} | all-to-all | bytes 2097152 | tf_op jit(solution)/shard_map/all_to_all | solution.py:94
  (488 shorter events, 277.9 us)
Async XLA Ops:
  6.5 584.2 %copy-start = (bf16[1024,1024]{1,0:T(8,128)(2,1)S(1)}, bf16[1024,1024]{1,0:T(8,128)(2,1)}, u32[]{:S(2)}) copy-start(bf16[1024,1024]{1,0:T(8,128)(2,1)} %param.9) | copy-start | bytes 6291460
  6.5 110.6 %all-gather.6.cloned.1.call-start = ((), (), s32[]{:S(2)}) async-start(), calls=%async_computation.4 | async-start | bytes 9437184 | tf_op jit(solution)/shard_map/all_gather | solution.py:44
  65.4 103.4 %all-gather.4.cloned.1.call-start = ((), (), s32[]{:S(2)}) async-start(), calls=%async_computation.3 | async-start | bytes 9437184 | tf_op jit(solution)/shard_map/all_gather | solution.py:43
  66.2 8.4 %copy-start.5 = (s32[64,16]{0,1:T(8,128)S(1)}, s32[64,16]{0,1:T(8,128)}, u32[]{:S(2)}) copy-start(s32[64,16]{0,1:T(8,128)} %param.10) | copy-start | bytes 12292
  66.2 8.4 %copy-start.6 = (s32[64]{0:T(128)S(1)}, s32[64]{0:T(128)}, u32[]{:S(2)}) copy-start(s32[64]{0:T(128)} %param.11) | copy-start | bytes 772
  70.1 19.3 %all-to-all-start.1 = ((bf16[16,512,64]{1,2,0:T(8,128)(2,1)}), bf16[16,512,64]{1,2,0:T(8,128)(2,1)S(1)}, u32[]{:S(2)}, u32[]{:S(2)}) async-start(bf16[16,512,64]{1,2,0:T(8,128)(2,1)} %fusion.14), calls=%async_computation.1 | async-start | bytes 2097152 | tf_op jit(solution)/shard_map/all_to_all | solution.py:28
  180.8 14.5 %copy-start.2 = (bf16[64,1,64,128]{3,2,1,0:T(8,128)(2,1)}, bf16[64,1,64,128]{3,2,1,0:T(8,128)(2,1)S(1)}, u32[]{:S(2)}) copy-start(bf16[64,1,64,128]{3,2,1,0:T(8,128)(2,1)S(1)} %get-tuple-element.202) | copy-start | bytes 3145732 | tf_op jit(solution)/shard_map/while
  199.3 3.2 copy-start.4
  205.0 14.5 %copy-start.2 = (bf16[64,1,64,128]{3,2,1,0:T(8,128)(2,1)}, bf16[64,1,64,128]{3,2,1,0:T(8,128)(2,1)S(1)}, u32[]{:S(2)}) copy-start(bf16[64,1,64,128]{3,2,1,0:T(8,128)(2,1)S(1)} %get-tuple-element.202) | copy-start | bytes 3145732 | tf_op jit(solution)/shard_map/while
  223.5 3.2 copy-start.4
  229.1 14.5 %copy-start.2 = (bf16[64,1,64,128]{3,2,1,0:T(8,128)(2,1)}, bf16[64,1,64,128]{3,2,1,0:T(8,128)(2,1)S(1)}, u32[]{:S(2)}) copy-start(bf16[64,1,64,128]{3,2,1,0:T(8,128)(2,1)S(1)} %get-tuple-element.202) | copy-start | bytes 3145732 | tf_op jit(solution)/shard_map/while
  247.6 3.2 copy-start.4
  253.2 14.6 %copy-start.2 = (bf16[64,1,64,128]{3,2,1,0:T(8,128)(2,1)}, bf16[64,1,64,128]{3,2,1,0:T(8,128)(2,1)S(1)}, u32[]{:S(2)}) copy-start(bf16[64,1,64,128]{3,2,1,0:T(8,128)(2,1)S(1)} %get-tuple-element.202) | copy-start | bytes 3145732 | tf_op jit(solution)/shard_map/while
  271.8 3.2 copy-start.4
  277.4 14.5 %copy-start.2 = (bf16[64,1,64,128]{3,2,1,0:T(8,128)(2,1)}, bf16[64,1,64,128]{3,2,1,0:T(8,128)(2,1)S(1)}, u32[]{:S(2)}) copy-start(bf16[64,1,64,128]{3,2,1,0:T(8,128)(2,1)S(1)} %get-tuple-element.202) | copy-start | bytes 3145732 | tf_op jit(solution)/shard_map/while
  295.9 3.2 copy-start.4
  301.5 14.5 %copy-start.2 = (bf16[64,1,64,128]{3,2,1,0:T(8,128)(2,1)}, bf16[64,1,64,128]{3,2,1,0:T(8,128)(2,1)S(1)}, u32[]{:S(2)}) copy-start(bf16[64,1,64,128]{3,2,1,0:T(8,128)(2,1)S(1)} %get-tuple-element.202) | copy-start | bytes 3145732 | tf_op jit(solution)/shard_map/while
  320.0 3.2 copy-start.4
  325.6 14.5 %copy-start.2 = (bf16[64,1,64,128]{3,2,1,0:T(8,128)(2,1)}, bf16[64,1,64,128]{3,2,1,0:T(8,128)(2,1)S(1)}, u32[]{:S(2)}) copy-start(bf16[64,1,64,128]{3,2,1,0:T(8,128)(2,1)S(1)} %get-tuple-element.202) | copy-start | bytes 3145732 | tf_op jit(solution)/shard_map/while
  344.1 3.2 copy-start.4
  349.7 14.5 %copy-start.2 = (bf16[64,1,64,128]{3,2,1,0:T(8,128)(2,1)}, bf16[64,1,64,128]{3,2,1,0:T(8,128)(2,1)S(1)}, u32[]{:S(2)}) copy-start(bf16[64,1,64,128]{3,2,1,0:T(8,128)(2,1)S(1)} %get-tuple-element.202) | copy-start | bytes 3145732 | tf_op jit(solution)/shard_map/while
  368.2 3.2 copy-start.4
  373.8 14.6 %copy-start.2 = (bf16[64,1,64,128]{3,2,1,0:T(8,128)(2,1)}, bf16[64,1,64,128]{3,2,1,0:T(8,128)(2,1)S(1)}, u32[]{:S(2)}) copy-start(bf16[64,1,64,128]{3,2,1,0:T(8,128)(2,1)S(1)} %get-tuple-element.202) | copy-start | bytes 3145732 | tf_op jit(solution)/shard_map/while
  392.4 3.2 copy-start.4
  398.0 14.6 %copy-start.2 = (bf16[64,1,64,128]{3,2,1,0:T(8,128)(2,1)}, bf16[64,1,64,128]{3,2,1,0:T(8,128)(2,1)S(1)}, u32[]{:S(2)}) copy-start(bf16[64,1,64,128]{3,2,1,0:T(8,128)(2,1)S(1)} %get-tuple-element.202) | copy-start | bytes 3145732 | tf_op jit(solution)/shard_map/while
  416.6 3.2 copy-start.4
  422.2 14.5 %copy-start.2 = (bf16[64,1,64,128]{3,2,1,0:T(8,128)(2,1)}, bf16[64,1,64,128]{3,2,1,0:T(8,128)(2,1)S(1)}, u32[]{:S(2)}) copy-start(bf16[64,1,64,128]{3,2,1,0:T(8,128)(2,1)S(1)} %get-tuple-element.202) | copy-start | bytes 3145732 | tf_op jit(solution)/shard_map/while
  446.3 14.5 %copy-start.2 = (bf16[64,1,64,128]{3,2,1,0:T(8,128)(2,1)}, bf16[64,1,64,128]{3,2,1,0:T(8,128)(2,1)S(1)}, u32[]{:S(2)}) copy-start(bf16[64,1,64,128]{3,2,1,0:T(8,128)(2,1)S(1)} %get-tuple-element.202) | copy-start | bytes 3145732 | tf_op jit(solution)/shard_map/while
  470.5 14.5 %copy-start.2 = (bf16[64,1,64,128]{3,2,1,0:T(8,128)(2,1)}, bf16[64,1,64,128]{3,2,1,0:T(8,128)(2,1)S(1)}, u32[]{:S(2)}) copy-start(bf16[64,1,64,128]{3,2,1,0:T(8,128)(2,1)S(1)} %get-tuple-element.202) | copy-start | bytes 3145732 | tf_op jit(solution)/shard_map/while
  494.6 14.5 %copy-start.2 = (bf16[64,1,64,128]{3,2,1,0:T(8,128)(2,1)}, bf16[64,1,64,128]{3,2,1,0:T(8,128)(2,1)S(1)}, u32[]{:S(2)}) copy-start(bf16[64,1,64,128]{3,2,1,0:T(8,128)(2,1)S(1)} %get-tuple-element.202) | copy-start | bytes 3145732 | tf_op jit(solution)/shard_map/while
  518.7 14.5 %copy-start.2 = (bf16[64,1,64,128]{3,2,1,0:T(8,128)(2,1)}, bf16[64,1,64,128]{3,2,1,0:T(8,128)(2,1)S(1)}, u32[]{:S(2)}) copy-start(bf16[64,1,64,128]{3,2,1,0:T(8,128)(2,1)S(1)} %get-tuple-element.202) | copy-start | bytes 3145732 | tf_op jit(solution)/shard_map/while
  542.9 14.5 %copy-start.2 = (bf16[64,1,64,128]{3,2,1,0:T(8,128)(2,1)}, bf16[64,1,64,128]{3,2,1,0:T(8,128)(2,1)S(1)}, u32[]{:S(2)}) copy-start(bf16[64,1,64,128]{3,2,1,0:T(8,128)(2,1)S(1)} %get-tuple-element.202) | copy-start | bytes 3145732 | tf_op jit(solution)/shard_map/while
  (39 other events, 74.6 us)
Sparse Core Ops, SparseCore 0:
  65.5 51.5 all-gather.5
  118.8 49.9 all-gather.3
where the time goes:
time: 605 us; the launch traced here: 600 us
  local copies, waits for them, and re-layouts  364 us (60%)
  matrix products  74.1 us (12%)
  waiting for transfers between devices  69.7 us (12%)
  blocking collectives  56.1 us (9%)
  other arithmetic  16.9 us (3%)
  between operations  13.5 us (2%)
    gather x16, local copies, waits for them, and re-layouts, attend(): far_v = far_values[far_ids]  115 us
    gather x16, local copies, waits for them, and re-layouts, attend(): far_k = far_keys[far_ids]  63.7 us
    gather x16, local copies, waits for them, and re-layouts, attend(): near_v = value_table[near_ids]  57.6 us
    while x4, local copies, waits for them, and re-layouts, on_device(): lax.map(attend, (queries.reshape(groups, 4, BLK, heads_dev, HD), local_id...  35.2 us
    dot_general x16, matrix products, attend(): jnp.einsum('qahe,qjhek->qhajk', query_blk, near_k, preferred_element_type...  34.2 us
    all_to_all x1, blocking collectives, on_device(): lax.all_to_all(keyval_proj, 'seq', split_axis=0, concat_axis=0, tiled=True)  33.9 us
    all_gather x1, waiting for transfers between devices, on_device(): lax.all_gather(key_table, 'cluster', axis=0, tiled=True)  33.7 us
    gather x16, local copies, waits for them, and re-layouts, attend(): near_k = key_table[near_ids]  24.9 us
  transfers between devices with their start and end apart: 3, of which 3 were waited for; matrix products, arithmetic and copies ran while one was open for 5% of the time, Pallas kernels for 0%

commit v1 on v0

v1 whole, which is shorter than its diff:
```python
import functools

import jax
import jax.numpy as jnp
from jax import lax
from jax.experimental import pallas as pl
from jax.experimental.pallas import tpu as pltpu
from jax.sharding import PartitionSpec as P

D = 1024
HEADS = 16
HD = 64
BLK = 128
KVB = 16
REMOTE = 4
NEAR = KVB - REMOTE
QB = 64
REQ = 16
CL = 8
SEQ = 16
OWN = 4
CH = 4
ROWS = BLK // CH
MESH = pl.DeviceIdType.MESH
F32 = jnp.float32
BF16 = jnp.bfloat16


def low_lanes(shape):
    return lax.broadcasted_iota(jnp.int32, shape, len(shape) - 1) < HD


def swap_halves(x):
    return pltpu.roll(x, HD, x.ndim - 1)


def body(
    idx_s,
    cnt_s,
    nodes,
    lists_v,
    w_hbm,
    o_ref,
    w_v,
    kvs,
    kvc0,
    kvc1,
    kvc2,
    kvc3,
    qs,
    qr,
    snd,
    far0,
    far1,
    far2,
    far3,
    lrecv,
    lsm,
    sc,
    acc_v,
    top_v,
    outs,
    ret,
    w_sem,
    l_ss,
    l_rs,
    kv_ss,
    kv_rs,
    q_ss,
    q_rs,
    z_ss,
    z_rs,
    r_ss,
    r_rs,
    own_sem,
    sm_sem,
):
    me = lax.axis_index("seq")
    mc = lax.axis_index("cluster")
    kvc = (kvc0, kvc1, kvc2, kvc3)
    far = (far0, far1, far2, far3)

    barrier = pltpu.get_barrier_semaphore()

    @pl.loop(1, SEQ)
    def _(d):
        pl.semaphore_signal(barrier, inc=1, device_id={"seq": lax.rem(me + d, SEQ)}, device_id_type=MESH)

    @pl.loop(1, CL)
    def _(d):
        pl.semaphore_signal(barrier, inc=1, device_id={"cluster": lax.rem(mc + d, CL)}, device_id_type=MESH)

    def w_copy(g):
        return pltpu.make_async_copy(
            w_hbm.at[:, pl.ds(pl.multiple_of(g * 384, 128), 384)], w_v.at[g], w_sem.at[g]
        )

    @pl.loop(0, 8)
    def _(g):
        w_copy(g).start()

    def project(c, first):
        x = nodes[:, pl.ds(c * ROWS, ROWS), :].reshape(OWN * ROWS, D)

        @pl.loop(0, 8)
        def _(g):
            if first:
                w_copy(g).wait()
            p = jnp.dot(x, w_v[g], preferred_element_type=F32)
            t0, t1, t2 = p[:, :128], p[:, 128:256], p[:, 256:]
            r0, r1 = swap_halves(t0), swap_halves(t1)
            low = low_lanes((OWN * ROWS, 128))
            kv0 = jnp.where(low, r0, r1).astype(BF16)
            kvs[2 * g, c] = kv0.reshape(OWN, ROWS, 128)
            kvs[2 * g + 1, c] = t2.astype(BF16).reshape(OWN, ROWS, 128)
            half = OWN * ROWS // 2
            lowh = low[:half]
            scale = HD**-0.5
            q0 = jnp.where(lowh, t0[:half], r0[half:]) * scale
            q1 = jnp.where(lowh, r1[:half], t1[half:]) * scale
            qs[2 * g, :, pl.ds(c * ROWS, ROWS), :] = q0.astype(BF16).reshape(2, ROWS, 128)
            qs[2 * g + 1, :, pl.ds(c * ROWS, ROWS), :] = q1.astype(BF16).reshape(2, ROWS, 128)

    def kv_copy(c, d):
        peer = lax.rem(me + d, SEQ)
        return pltpu.make_async_remote_copy(
            src_ref=kvs.at[peer, c],
            dst_ref=kvc[c].at[pl.ds(OWN * me, OWN)],
            send_sem=kv_ss.at[c, d],
            recv_sem=kv_rs.at[c, d],
            device_id={"seq": peer},
            device_id_type=MESH,
        )

    def kv_own(c):
        return pltpu.make_async_copy(kvs.at[me, c], kvc[c].at[pl.ds(OWN * me, OWN)], own_sem.at[c])

    def q_copy(i, d):
        peer = lax.rem(me + d, SEQ)
        return pltpu.make_async_remote_copy(
            src_ref=qs.at[peer, i],
            dst_ref=qr.at[i, me],
            send_sem=q_ss.at[i, d],
            recv_sem=q_rs.at[i, d],
            device_id={"seq": peer},
            device_id_type=MESH,
        )

    def q_own(i):
        return pltpu.make_async_copy(qs.at[me, i], qr.at[i, me], own_sem.at[CH + i])

    def list_copy(d):
        peer = lax.rem(mc + d, CL)
        return pltpu.make_async_remote_copy(
            src_ref=lists_v.at[peer],
            dst_ref=lrecv.at[CL - d],
            send_sem=l_ss.at[d],
            recv_sem=l_rs.at[d],
            device_id={"cluster": peer},
            device_id_type=MESH,
        )

    def z_copy(c, d):
        return pltpu.make_async_remote_copy(
            src_ref=snd.at[c, d],
            dst_ref=far[c].at[pl.ds(REQ * mc, REQ)],
            send_sem=z_ss.at[c, d],
            recv_sem=z_rs.at[c, d],
            device_id={"cluster": lax.rem(mc + d, CL)},
            device_id_type=MESH,
        )

    def ret_copy(i, peer, d):
        return pltpu.make_async_remote_copy(
            src_ref=outs.at[i, peer],
            dst_ref=ret.at[i, me],
            send_sem=r_ss.at[i, d],
            recv_sem=r_rs.at[i, d],
            device_id={"seq": peer},
            device_id_type=MESH,
        )

    def ret_own(i):
        return pltpu.make_async_copy(outs.at[i, me], ret.at[i, me], own_sem.at[CH + 2 + i])

    def start_kv(c):
        kv_own(c).start()

        @pl.loop(1, SEQ)
        def _(d):
            kv_copy(c, d).start()

    def start_q(i):
        q_own(i).start()

        @pl.loop(1, SEQ)
        def _(d):
            q_copy(i, d).start()

    def wait_kv(c):
        kv_own(c).wait()

        @pl.loop(1, SEQ)
        def _(d):
            kv_copy(c, d).wait()

    def wait_q(i):
        q_own(i).wait()

        @pl.loop(1, SEQ)
        def _(d):
            q_copy(i, d).wait()

    def pack(c):
        @pl.loop(1, CL)
        def _(d):
            for r in range(REQ):
                snd[c, d, r] = kvc[c][lsm[d, 0, r]]
            z_copy(c, d).start()

    project(0, True)
    pl.semaphore_wait(barrier, SEQ + CL - 2)

    @pl.loop(1, CL)
    def _(d):
        list_copy(d).start()

    start_kv(0)
    project(1, False)
    start_kv(1)
    project(2, False)
    project(3, False)

    @pl.loop(1, CL)
    def _(d):
        list_copy(d).wait()

    sm_copy = pltpu.make_async_copy(lrecv.at[pl.ds(1, CL - 1)], lsm.at[pl.ds(1, CL - 1)], sm_sem)
    sm_copy.start()
    sm_copy.wait()

    wait_kv(0)
    start_kv(2)
    pack(0)
    wait_kv(1)
    start_kv(3)
    pack(1)
    wait_kv(2)
    start_q(0)
    pack(2)
    wait_kv(3)
    start_q(1)
    pack(3)

    def block_of(bufs, b):
        return [bufs[c][b] for c in range(CH)]

    def pair_of(bufs, qb, j):
        return jnp.concatenate(
            block_of(bufs, idx_s[qb * KVB + j]) + block_of(bufs, idx_s[qb * KVB + j + 1]), axis=0
        )

    def score(q, kv):
        return lax.dot_general(q, kv, (((1,), (1,)), ((), ())), preferred_element_type=F32)

    def weigh(s, m, kv):
        p = jnp.exp(s - m).astype(BF16)
        v1 = jnp.where(low_lanes(kv.shape), jnp.ones_like(kv), kv)
        return jnp.dot(p, v1, preferred_element_type=F32)

    def queries(i, s):
        qp = qr[i, s]
        low = low_lanes(qp.shape)
        left = jnp.where(low, qp, jnp.zeros_like(qp))
        right = jnp.where(low, swap_halves(qp.astype(F32)), 0.0).astype(BF16)
        return left, right

    def near(i):
        @pl.loop(0, SEQ)
        def _(s):
            for half, q in enumerate(queries(i, s)):
                qb = s * OWN + i + 2 * half
                top = None
                for jj in range(NEAR // 2):
                    sco = score(q, pair_of(kvc, qb, 2 * jj))
                    sc[half, jj] = sco
                    t = jnp.maximum(sco[:, :BLK], sco[:, BLK:])
                    top = t if top is None else jnp.maximum(top, t)
                m = jnp.max(top, axis=1, keepdims=True)
                acc = None
                for jj in range(NEAR // 2):
                    a = weigh(sc[half, jj], m, pair_of(kvc, qb, 2 * jj))
                    acc = a if acc is None else acc + a
                acc_v[i, s, half] = acc
                top_v[i, s, half] = jnp.broadcast_to(m, (BLK, 128))

    def distant(i):
        @pl.loop(0, SEQ)
        def _(t):
            s = lax.rem(me + t, SEQ)
            packed = []
            for half, q in enumerate(queries(i, s)):
                qb = s * OWN + i + 2 * half
                valid = cnt_s[qb]
                scores, kvs_ = [], []
                mt = top_v[i, s, half]
                m = mt
                for jj in range(REMOTE // 2):
                    kv = pair_of(far, qb, NEAR + 2 * jj)
                    sco = score(q, kv)
                    for part in range(2):
                        piece = sco[:, part * BLK : (part + 1) * BLK]
                        piece = jnp.where(NEAR + 2 * jj + part < valid, piece, -1e30)
                        scores.append(piece)
                        m = jnp.maximum(m, piece)
                    kvs_.append(kv)
                m = jnp.max(m, axis=1, keepdims=True)
                acc = acc_v[i, s, half] * jnp.exp(mt - m)
                for jj in range(REMOTE // 2):
                    both = jnp.concatenate(scores[2 * jj : 2 * jj + 2], axis=1)
                    acc = acc + weigh(both, m, kvs_[jj])
                packed.append(acc)
            low = low_lanes((BLK, 128))
            left, right = packed
            lsw, rsw = swap_halves(left), swap_halves(right)
            value = jnp.where(low, lsw, right)
            total = jnp.where(low, left, rsw)
            outs[i, s] = (value / total).astype(BF16)

            @pl.when(t > 0)
            def _():
                ret_copy(i, s, t).start()

    wait_q(0)
    near(0)
    wait_q(1)
    near(1)

    for c in range(CH):

        @pl.loop(1, CL)
        def _(d, c=c):
            z_copy(c, d).wait()

    for i in range(2):
        distant(i)
        ret_own(i).start()

    for i in range(2):
        ret_own(i).wait()

        @pl.loop(1, SEQ)
        def _(d, i=i):
            ret_copy(i, lax.rem(me + d, SEQ), d).wait()

    for g in range(HEADS // 2):
        for i in range(2):
            a = ret[i, 2 * g].astype(F32)
            b = ret[i, 2 * g + 1].astype(F32)
            low = low_lanes(a.shape)
            o_ref[i, :, g * 128 : (g + 1) * 128] = jnp.where(low, a, swap_halves(b)).astype(BF16)
            o_ref[2 + i, :, g * 128 : (g + 1) * 128] = jnp.where(low, swap_halves(a), b).astype(BF16)


def request_lists(kv_ids, cluster):
    named = kv_ids[:, NEAR:]
    blocks = jnp.arange(CL * QB, dtype=jnp.int32)
    onehot = named.reshape(-1, 1) == blocks[None, :]
    present = jnp.any(onehot, axis=0).reshape(CL, QB)
    inner = jnp.arange(QB, dtype=jnp.int32)
    rank = jnp.sum(
        jnp.where(present[:, None, :] & (inner[None, None, :] < inner[None, :, None]), 1, 0), axis=2
    )
    slot = jnp.arange(REQ, dtype=jnp.int32)
    hit = present[:, None, :] & (rank[:, None, :] == slot[None, :, None])
    lists = jnp.sum(jnp.where(hit, inner[None, None, :], 0), axis=2)
    place = (rank + REQ * jnp.arange(CL, dtype=jnp.int32)[:, None]).reshape(-1)
    far = jnp.sum(jnp.where(onehot, place[None, :], 0), axis=1).reshape(QB, REMOTE)
    idx = jnp.concatenate([kv_ids[:, :NEAR] - cluster * QB, far], axis=1).reshape(-1)
    lists = jnp.broadcast_to(jnp.pad(lists, ((0, 0), (0, 128 - REQ)))[:, None, :], (CL, 8, 128))
    return idx, lists


def on_device(nodes, w_qkv, w_out, kv_ids, counts):
    idx, lists = request_lists(kv_ids, lax.axis_index("cluster"))
    vm = pl.BlockSpec(memory_space=pltpu.VMEM)
    sm = pl.BlockSpec(memory_space=pltpu.SMEM)
    dma = pltpu.SemaphoreType.DMA
    attended = pl.pallas_call(
        body,
        out_shape=jax.ShapeDtypeStruct((OWN, BLK, D), BF16),
        in_specs=[sm, sm, vm, vm, pl.BlockSpec(memory_space=pl.ANY)],
        out_specs=vm,
        scratch_shapes=[
            pltpu.VMEM((8, D, 384), BF16),
            pltpu.VMEM((HEADS, CH, OWN, ROWS, 128), BF16),
            *[pltpu.VMEM((QB, ROWS, 128), BF16) for _ in range(CH)],
            pltpu.VMEM((HEADS, 2, BLK, 128), BF16),
            pltpu.VMEM((2, SEQ, BLK, 128), BF16),
            pltpu.VMEM((CH, CL, REQ, ROWS, 128), BF16),
            *[pltpu.VMEM((CL * REQ, ROWS, 128), BF16) for _ in range(CH)],
            pltpu.VMEM((CL, 8, 128), jnp.int32),
            pltpu.SMEM((CL, 8, 128), jnp.int32),
            pltpu.VMEM((2, NEAR // 2, BLK, 2 * BLK), F32),
            pltpu.VMEM((2, SEQ, 2, BLK, 128), F32),
            pltpu.VMEM((2, SEQ, 2, BLK, 128), F32),
            pltpu.VMEM((2, SEQ, BLK, 128), BF16),
            pltpu.VMEM((2, SEQ, BLK, 128), BF16),
            dma((8,)),
            dma((CL,)),
            dma((CL,)),
            dma((CH, SEQ)),
            dma((CH, SEQ)),
            dma((2, SEQ)),
            dma((2, SEQ)),
            dma((CH, CL)),
            dma((CH, CL)),
            dma((2, SEQ)),
            dma((2, SEQ)),
            dma((CH + 4,)),
            dma(()),
        ],
        compiler_params=pltpu.CompilerParams(
            collective_id=0, has_side_effects=True, vmem_limit_bytes=60 << 20
        ),
        name="sublayer",
    )(idx, counts, nodes.reshape(OWN, BLK, D), lists, w_qkv)
    return jnp.dot(attended.reshape(OWN * BLK, D), w_out, preferred_element_type=F32).astype(BF16)


def solution(mesh):
    placed = (P(("cluster", "seq"), None), P(), P(), P("cluster", None), P("cluster"))
    return jax.shard_map(
        on_device,
        mesh=mesh,
        in_specs=placed,
        out_specs=P(("cluster", "seq"), None),
        check_vma=False,
    )
```

time: 605 us -> 115 us (0.19)
  the two profiles are of different devices: /device:TPU:1 before, /device:TPU:92 now
where the time goes in v1:
time: 115 us
  Pallas kernels  107 us (93%)
  matrix products  3.45 us (3%)
  local copies, waits for them, and re-layouts  2.76 us (2%)
  other arithmetic  1.59 us (1%)
    pallas_call x1, Pallas kernels, on_device(): pl.pallas_call(body, out_shape=jax.ShapeDtypeStruct((OWN, BLK, D), BF16),...  107 us
    dot_general x1, matrix products, on_device(): jnp.dot(attended.reshape(OWN * BLK, D), w_out, preferred_element_type=F32)  3.45 us

profile of v1, /device:TPU:92, one launch (start us, length us, event | category | flops | bytes accessed | tf_op | source)
XLA Modules:
  0.0 115.1 jit_solution(15199502497796879851)
XLA Ops:
  0.0 0.0 copy-start
  0.0 0.8 slice.7
  0.8 0.7 slice_subtract_fusion
  1.6 0.1 copy.9
  1.7 0.1 eq.28
  1.8 0.2 fusion
  1.9 0.1 and.24
  2.0 0.2 select_reduce_fusion.1
  2.2 0.2 select_reduce_fusion.2
  2.4 0.1 broadcast_add_fusion
  2.5 0.1 add.19
  2.6 0.2 select_reduce_fusion
  2.8 0.6 broadcast_in_dim.51.lists_v
  3.4 0.1 reshape.49
  3.5 0.1 copy.10
  3.6 0.1 copy.11
  3.7 0.7 reshape.50.idx_s
  4.4 107.3 %sublayer.1 = bf16[4,128,1024]{2,1,0:T(8,128)(2,1)} custom-call(s32[1024]{0:T(1024)} %reshape.50.idx_s, s32[64]{0:T(128)} %cnt_s.1, bf16[4,128,1024]{2,1,0:T(8,128)(2,1)} %bitcast.4, s32[8,8,128]{2,1,0:T(8,128)} %broadcast_in_dim.51.lists_v, bf16[1024,3072]{1,0:T(8,128)(2,1)} %w_hbm.1), custom_call_target="tpu_custom_call" | custom-call | tf_op jit(solution)/shard_map/sublayer/pallas_call | solution.py:389
  111.7 0.0 copy-done
  111.7 3.4 %convolution_convert_fusion = bf16[512,1024]{1,0:T(8,128)(2,1)} fusion(bf16[512,1024]{1,0:T(8,128)(2,1)} %bitcast.5, bf16[1024,1024]{1,0:T(8,128)(2,1)S(1)} %copy-done), kind=kOutput, calls=%fused_computation | convolution fusion | flops 1074266112 | bytes 4194304 | tf_op jit(solution)/shard_map/dot_general | solution.py:428
  (4 shorter events, 0.0 us)
Async XLA Ops:
  0.0 111.7 %copy-start = (bf16[1024,1024]{1,0:T(8,128)(2,1)S(1)}, bf16[1024,1024]{1,0:T(8,128)(2,1)}, u32[]{:S(2)}) copy-start(bf16[1024,1024]{1,0:T(8,128)(2,1)} %param.7) | copy-start | bytes 6291460

commit v2 on v1

v2 whole, which is shorter than its diff:
```python
import functools

import jax
import jax.numpy as jnp
from jax import lax
from jax.experimental import pallas as pl
from jax.experimental.pallas import tpu as pltpu
from jax.sharding import PartitionSpec as P

D = 1024
HEADS = 16
HD = 64
BLK = 128
KVB = 16
REMOTE = 4
NEAR = KVB - REMOTE
QB = 64
REQ = 16
CL = 8
SEQ = 16
OWN = 4
CH = 4
ROWS = BLK // CH
GROUPS = 4
WCOL = 3 * D // GROUPS
SIDE = 8
MESH = pl.DeviceIdType.MESH
F32 = jnp.float32
BF16 = jnp.bfloat16


def low_lanes(shape):
    return lax.broadcasted_iota(jnp.int32, shape, len(shape) - 1) < HD


def swap_halves(x):
    return pltpu.roll(x, HD, x.ndim - 1)


def body(
    ids_s,
    cnt_s,
    nodes,
    ids_v,
    w_hbm,
    o_ref,
    w_v,
    kvs,
    kvc0,
    kvc1,
    kvc2,
    kvc3,
    qs,
    qr,
    snd,
    far0,
    far1,
    far2,
    far3,
    lsend,
    lrecv,
    lsm,
    far_v,
    far_s,
    sc,
    acc_v,
    top_v,
    outs,
    ret,
    w_sem,
    l_ss,
    l_rs,
    kv_ss,
    kv_rs,
    q_ss,
    q_rs,
    z_ss,
    z_rs,
    r_ss,
    r_rs,
    own_sem,
    sm_sem,
):
    me = lax.axis_index("seq")
    mc = lax.axis_index("cluster")
    kvc = (kvc0, kvc1, kvc2, kvc3)
    far = (far0, far1, far2, far3)

    barrier = pltpu.get_barrier_semaphore()

    @pl.loop(1, SEQ)
    def _(d):
        pl.semaphore_signal(barrier, inc=1, device_id={"seq": lax.rem(me + d, SEQ)}, device_id_type=MESH)

    @pl.loop(1, CL)
    def _(d):
        pl.semaphore_signal(barrier, inc=1, device_id={"cluster": lax.rem(mc + d, CL)}, device_id_type=MESH)

    def w_copy(g):
        return pltpu.make_async_copy(
            w_hbm.at[:, pl.ds(pl.multiple_of(g * WCOL, 128), WCOL)], w_v.at[g], w_sem.at[g]
        )

    @pl.loop(0, GROUPS)
    def _(g):
        w_copy(g).start()

    @pl.loop(0, GROUPS)
    def _(g):
        w_copy(g).wait()
        p = jnp.dot(nodes[...], w_v[g], preferred_element_type=F32)
        low = low_lanes((OWN * BLK, 128))
        half = OWN * BLK // 2
        scale = HD**-0.5
        for k in range(2):
            t0, t1, t2 = (p[:, 384 * k + 128 * n : 384 * k + 128 * n + 128] for n in range(3))
            r0, r1 = swap_halves(t0), swap_halves(t1)
            h0 = 4 * g + 2 * k
            kv0 = jnp.where(low, r0, r1).astype(BF16).reshape(OWN, BLK, 128)
            kv1 = t2.astype(BF16).reshape(OWN, BLK, 128)
            for c in range(CH):
                kvs[h0, c] = kv0[:, c * ROWS : (c + 1) * ROWS]
                kvs[h0 + 1, c] = kv1[:, c * ROWS : (c + 1) * ROWS]
            q0 = jnp.where(low[:half], t0[:half], r0[half:]) * scale
            q1 = jnp.where(low[:half], r1[:half], t1[half:]) * scale
            qs[h0] = q0.astype(BF16).reshape(2, BLK, 128)
            qs[h0 + 1] = q1.astype(BF16).reshape(2, BLK, 128)

    def kv_copy(c, d):
        peer = lax.rem(me + d, SEQ)
        return pltpu.make_async_remote_copy(
            src_ref=kvs.at[peer, c],
            dst_ref=kvc[c].at[pl.ds(OWN * me, OWN)],
            send_sem=kv_ss.at[c, d],
            recv_sem=kv_rs.at[c, d],
            device_id={"seq": peer},
            device_id_type=MESH,
        )

    def kv_own(c):
        return pltpu.make_async_copy(kvs.at[me, c], kvc[c].at[pl.ds(OWN * me, OWN)], own_sem.at[c])

    def q_copy(i, d):
        peer = lax.rem(me + d, SEQ)
        return pltpu.make_async_remote_copy(
            src_ref=qs.at[peer, i],
            dst_ref=qr.at[i, me],
            send_sem=q_ss.at[i, d],
            recv_sem=q_rs.at[i, d],
            device_id={"seq": peer},
            device_id_type=MESH,
        )

    def q_own(i):
        return pltpu.make_async_copy(qs.at[me, i], qr.at[i, me], own_sem.at[CH + i])

    def list_copy(d):
        peer = lax.rem(mc + d, CL)
        return pltpu.make_async_remote_copy(
            src_ref=lsend.at[peer],
            dst_ref=lrecv.at[CL - d],
            send_sem=l_ss.at[d],
            recv_sem=l_rs.at[d],
            device_id={"cluster": peer},
            device_id_type=MESH,
        )

    def z_copy(c, d):
        return pltpu.make_async_remote_copy(
            src_ref=snd.at[c, d],
            dst_ref=far[c].at[pl.ds(REQ * mc, REQ)],
            send_sem=z_ss.at[c, d],
            recv_sem=z_rs.at[c, d],
            device_id={"cluster": lax.rem(mc + d, CL)},
            device_id_type=MESH,
        )

    def ret_copy(i, peer, d):
        return pltpu.make_async_remote_copy(
            src_ref=outs.at[i, peer],
            dst_ref=ret.at[i, me],
            send_sem=r_ss.at[i, d],
            recv_sem=r_rs.at[i, d],
            device_id={"seq": peer},
            device_id_type=MESH,
        )

    def ret_own(i):
        return pltpu.make_async_copy(outs.at[i, me], ret.at[i, me], own_sem.at[CH + 2 + i])

    def start(own, copy):
        own.start()

        @pl.loop(1, SEQ)
        def _(d):
            copy(d).start()

    def start_after(done, own, copy):
        own.start()

        @pl.loop(1, SEQ)
        def _(d):
            done(d).wait_send()
            copy(d).start()

    def landed(own, copy):
        own.wait()

        @pl.loop(1, SEQ)
        def _(d):
            copy(d).wait_recv()

    def kv(c):
        return functools.partial(kv_copy, c)

    def qq(i):
        return functools.partial(q_copy, i)

    def pack(c):
        @pl.loop(1, CL)
        def _(d):
            for r in range(REQ):
                snd[c, d, r] = kvc[c][lsm[d, r, 0] & (QB - 1)]
            z_copy(c, d).start()

    pl.semaphore_wait(barrier, SEQ + CL - 2)
    start(kv_own(0), kv(0))

    lane = lax.broadcasted_iota(jnp.int32, (QB, CL * QB), 1)
    hits = [ids_v[:, NEAR + j : NEAR + j + 1] == lane for j in range(REMOTE)]
    named = jnp.where(hits[0] | hits[1] | hits[2] | hits[3], 1.0, 0.0)
    present = jnp.max(named, axis=0, keepdims=True)
    present = jnp.broadcast_to(present, (8, CL * QB))
    lane8 = lax.broadcasted_iota(jnp.int32, (8, CL * QB), 1)
    inner = lane8 % QB
    rank = present
    step = 1
    while step < QB:
        rank = rank + jnp.where(inner >= step, pltpu.roll(rank, step, 1), 0.0)
        step *= 2
    rank = rank - present
    place = rank + (lane8 // QB * REQ).astype(F32)
    for j in range(REMOTE):
        at = jnp.sum(jnp.where(hits[j], place[:1], 0.0), axis=1, keepdims=True)
        far_v[j] = jnp.broadcast_to(at, (QB, 128)).astype(jnp.int32)
    slot = lax.broadcasted_iota(jnp.int32, (REQ, CL * QB), 0).astype(F32)
    wanted = jnp.where((slot == rank[:1]) & (present[:1] > 0.5), inner[:1].astype(F32), 0.0)
    lane_r = lax.broadcasted_iota(jnp.int32, (REQ, 128), 1)
    for p in range(CL):
        tile = wanted[:, p // 2 * 128 : p // 2 * 128 + 128]
        mine = jnp.where((lane_r >= HD) == (p % 2 == 1), tile, 0.0)
        block = jnp.sum(mine, axis=1, keepdims=True)
        lsend[p] = jnp.broadcast_to(block, (REQ, 128)).astype(jnp.int32)

    @pl.loop(1, CL)
    def _(d):
        list_copy(d).start()

    far_copy = pltpu.make_async_copy(far_v, far_s, sm_sem.at[1])
    far_copy.start()

    start_after(kv(0), kv_own(1), kv(1))

    @pl.loop(1, CL)
    def _(d):
        list_copy(d).wait()

    sm_copy = pltpu.make_async_copy(
        lrecv.at[pl.ds(1, CL - 1)], lsm.at[pl.ds(1, CL - 1)], sm_sem.at[0]
    )
    sm_copy.start()
    sm_copy.wait()
    far_copy.wait()

    landed(kv_own(0), kv(0))
    pack(0)
    start_after(kv(1), kv_own(2), kv(2))
    landed(kv_own(1), kv(1))
    pack(1)
    start_after(kv(2), kv_own(3), kv(3))
    landed(kv_own(2), kv(2))
    pack(2)
    start_after(kv(3), q_own(0), qq(0))
    landed(kv_own(3), kv(3))
    pack(3)
    start_after(qq(0), q_own(1), qq(1))

    def block_of(bufs, b):
        return [bufs[c][b] for c in range(CH)]

    def pair_of(bufs, b0, b1):
        return jnp.concatenate(block_of(bufs, b0) + block_of(bufs, b1), axis=0)

    def near_pair(qb, j):
        return pair_of(kvc, ids_s[qb, j] & (QB - 1), ids_s[qb, j + 1] & (QB - 1))

    def far_pair(qb, j):
        last = CL * REQ - 1
        return pair_of(far, far_s[j, qb, 0] & last, far_s[j + 1, qb, 0] & last)

    def score(q, kv):
        return lax.dot_general(q, kv, (((1,), (1,)), ((), ())), preferred_element_type=F32)

    def weigh(s, m, kv):
        p = jnp.exp(s - m).astype(BF16)
        v1 = jnp.where(low_lanes(kv.shape), jnp.ones_like(kv), kv)
        return jnp.dot(p, v1, preferred_element_type=F32)

    def queries(i, s):
        qp = qr[i, s]
        low = low_lanes(qp.shape)
        left = jnp.where(low, qp, jnp.zeros_like(qp))
        right = jnp.where(low, swap_halves(qp.astype(F32)), 0.0).astype(BF16)
        return left, right

    def items_of(i, first):
        items = []
        for u in range(SIDE // 2):
            s = lax.rem(me + first + u, SEQ)
            for half, q in enumerate(queries(i, s)):
                items.append((s, half, q, s * OWN + i + 2 * half))
        return items

    def near(i):
        @pl.loop(0, 2 * SEQ // SIDE)
        def _(t):
            items = items_of(i, t * (SIDE // 2))
            tops = [None] * SIDE
            for jj in range(NEAR // 2):
                for g, (s, half, q, qb) in enumerate(items):
                    sco = score(q, near_pair(qb, 2 * jj))
                    sc[g, jj] = sco
                    top = jnp.maximum(sco[:, :BLK], sco[:, BLK:])
                    tops[g] = top if jj == 0 else jnp.maximum(tops[g], top)
            tops = [jnp.max(top, axis=1, keepdims=True) for top in tops]
            accs = [None] * SIDE
            for jj in range(NEAR // 2):
                for g, (s, half, q, qb) in enumerate(items):
                    a = weigh(sc[g, jj], tops[g], near_pair(qb, 2 * jj))
                    accs[g] = a if jj == 0 else accs[g] + a
            for g, (s, half, q, qb) in enumerate(items):
                acc_v[i, s, half] = accs[g]
                top_v[i, s, half] = jnp.broadcast_to(tops[g], (BLK, 128))

    def distant(i):
        @pl.loop(0, 2 * SEQ // SIDE)
        def _(t):
            items = items_of(i, t * (SIDE // 2))
            pairs = [[far_pair(qb, 2 * jj) for jj in range(REMOTE // 2)] for _, _, _, qb in items]
            scores, tops, accs = [], [], []
            for g, (s, half, q, qb) in enumerate(items):
                pieces = []
                for jj in range(REMOTE // 2):
                    sco = score(q, pairs[g][jj])
                    for part in range(2):
                        piece = sco[:, part * BLK : (part + 1) * BLK]
                        valid = NEAR + 2 * jj + part < cnt_s[qb]
                        pieces.append(jnp.where(valid, piece, -1e30))
                scores.append(pieces)
            for g, (s, half, q, qb) in enumerate(items):
                m = top_v[i, s, half]
                for piece in scores[g]:
                    m = jnp.maximum(m, piece)
                tops.append(jnp.max(m, axis=1, keepdims=True))
            for g, (s, half, q, qb) in enumerate(items):
                acc = acc_v[i, s, half] * jnp.exp(top_v[i, s, half] - tops[g])
                for jj in range(REMOTE // 2):
                    both = jnp.concatenate(scores[g][2 * jj : 2 * jj + 2], axis=1)
                    acc = acc + weigh(both, tops[g], pairs[g][jj])
                accs.append(acc)
            low = low_lanes((BLK, 128))
            for u in range(SIDE // 2):
                s = items[2 * u][0]
                left, right = accs[2 * u : 2 * u + 2]
                lsw, rsw = swap_halves(left), swap_halves(right)
                value = jnp.where(low, lsw, right)
                total = jnp.where(low, left, rsw)
                outs[i, s] = (value / total).astype(BF16)

            for u in range(SIDE // 2):
                d = t * (SIDE // 2) + u

                @pl.when(d > 0)
                def _(d=d):
                    ret_copy(i, lax.rem(me + d, SEQ), d).start()

    landed(q_own(0), qq(0))
    near(0)
    landed(q_own(1), qq(1))
    near(1)

    for c in range(CH):

        @pl.loop(1, CL)
        def _(d, c=c):
            z_copy(c, d).wait()

    for i in range(2):
        distant(i)
        ret_own(i).start()

    @pl.loop(1, SEQ)
    def _(d):
        q_copy(1, d).wait_send()

    for i in range(2):
        ret_own(i).wait()

        @pl.loop(1, SEQ)
        def _(d, i=i):
            ret_copy(i, lax.rem(me + d, SEQ), d).wait()

    for g in range(HEADS // 2):
        for i in range(2):
            a = ret[i, 2 * g].astype(F32)
            b = ret[i, 2 * g + 1].astype(F32)
            low = low_lanes(a.shape)
            o_ref[i, :, g * 128 : (g + 1) * 128] = jnp.where(low, a, swap_halves(b)).astype(BF16)
            o_ref[2 + i, :, g * 128 : (g + 1) * 128] = jnp.where(low, swap_halves(a), b).astype(BF16)


def on_device(nodes, w_qkv, w_out, kv_ids, counts):
    vm = pl.BlockSpec(memory_space=pltpu.VMEM)
    sm = pl.BlockSpec(memory_space=pltpu.SMEM)
    dma = pltpu.SemaphoreType.DMA
    attended = pl.pallas_call(
        body,
        out_shape=jax.ShapeDtypeStruct((OWN, BLK, D), BF16),
        in_specs=[sm, sm, vm, vm, pl.BlockSpec(memory_space=pl.ANY)],
        out_specs=vm,
        scratch_shapes=[
            pltpu.VMEM((GROUPS, D, WCOL), BF16),
            pltpu.VMEM((HEADS, CH, OWN, ROWS, 128), BF16),
            *[pltpu.VMEM((QB, ROWS, 128), BF16) for _ in range(CH)],
            pltpu.VMEM((HEADS, 2, BLK, 128), BF16),
            pltpu.VMEM((2, SEQ, BLK, 128), BF16),
            pltpu.VMEM((CH, CL, REQ, ROWS, 128), BF16),
            *[pltpu.VMEM((CL * REQ, ROWS, 128), BF16) for _ in range(CH)],
            pltpu.VMEM((CL, REQ, 128), jnp.int32),
            pltpu.VMEM((CL, REQ, 128), jnp.int32),
            pltpu.SMEM((CL, REQ, 128), jnp.int32),
            pltpu.VMEM((REMOTE, QB, 128), jnp.int32),
            pltpu.SMEM((REMOTE, QB, 128), jnp.int32),
            pltpu.VMEM((SIDE, NEAR // 2, BLK, 2 * BLK), F32),
            pltpu.VMEM((2, SEQ, 2, BLK, 128), F32),
            pltpu.VMEM((2, SEQ, 2, BLK, 128), F32),
            pltpu.VMEM((2, SEQ, BLK, 128), BF16),
            pltpu.VMEM((2, SEQ, BLK, 128), BF16),
            dma((GROUPS,)),
            dma((CL,)),
            dma((CL,)),
            dma((CH, SEQ)),
            dma((CH, SEQ)),
            dma((2, SEQ)),
            dma((2, SEQ)),
            dma((CH, CL)),
            dma((CH, CL)),
            dma((2, SEQ)),
            dma((2, SEQ)),
            dma((CH + 4,)),
            dma((2,)),
        ],
        compiler_params=pltpu.CompilerParams(
            collective_id=0, has_side_effects=True, vmem_limit_bytes=60 << 20
        ),
        name="sublayer",
    )(kv_ids, counts, nodes, kv_ids, w_qkv)
    return jnp.dot(attended.reshape(OWN * BLK, D), w_out, preferred_element_type=F32).astype(BF16)


def solution(mesh):
    placed = (P(("cluster", "seq"), None), P(), P(), P("cluster", None), P("cluster"))
    return jax.shard_map(
        on_device,
        mesh=mesh,
        in_specs=placed,
        out_specs=P(("cluster", "seq"), None),
        check_vma=False,
    )
```

time: 115 us -> 95.8 us (0.83)
  the two profiles are of different devices: /device:TPU:92 before, /device:TPU:1 now
where the time goes in v2:
time: 95.8 us; the launch traced here: 95.1 us
  Pallas kernels  90.1 us (94%)
  matrix products  3.45 us (4%)
  local copies, waits for them, and re-layouts  1.55 us (2%)
    pallas_call x1, Pallas kernels, on_device(): pl.pallas_call(body, out_shape=jax.ShapeDtypeStruct((OWN, BLK, D), BF16),...  90.1 us
    dot_general x1, matrix products, on_device(): jnp.dot(attended.reshape(OWN * BLK, D), w_out, preferred_element_type=F32)  3.45 us

profile of v2, /device:TPU:1, one launch (start us, length us, event | category | flops | bytes accessed | tf_op | source)
XLA Modules:
  0.0 95.1 jit_solution(9112913136061434011)
XLA Ops:
  0.0 0.0 copy-start
  0.0 1.5 %copy.6.ids_s.ids_v = s32[64,16]{1,0:T(8,128)} copy(s32[64,16]{0,1:T(8,128)} %param.8) | data formatting | bytes 8192 | tf_op args[3]
  1.5 90.1 %sublayer.1 = bf16[4,128,1024]{2,1,0:T(8,128)(2,1)} custom-call(s32[64,16]{1,0:T(8,128)} %copy.6.ids_s.ids_v, s32[64]{0:T(128)} %cnt_s.1, bf16[512,1024]{1,0:T(8,128)(2,1)} %nodes.1, s32[64,16]{1,0:T(8,128)} %copy.6.ids_s.ids_v, bf16[1024,3072]{1,0:T(8,128)(2,1)} %w_hbm.1), custom_call_target="tpu_custom_call" | custom-call | tf_op jit(solution)/shard_map/sublayer/pallas_call | solution.py:426
  91.6 0.0 copy-done
  91.7 3.4 %convolution_convert_fusion = bf16[512,1024]{1,0:T(8,128)(2,1)} fusion(bf16[512,1024]{1,0:T(8,128)(2,1)} %bitcast.3, bf16[1024,1024]{1,0:T(8,128)(2,1)S(1)} %copy-done), kind=kOutput, calls=%fused_computation | convolution fusion | flops 1074266112 | bytes 4194304 | tf_op jit(solution)/shard_map/dot_general | solution.py:468
Async XLA Ops:
  0.0 91.6 %copy-start = (bf16[1024,1024]{1,0:T(8,128)(2,1)S(1)}, bf16[1024,1024]{1,0:T(8,128)(2,1)}, u32[]{:S(2)}) copy-start(bf16[1024,1024]{1,0:T(8,128)(2,1)} %param.7) | copy-start | bytes 6291460

commit v3 on v2

--- a/solution.py
+++ b/solution.py
@@ -19,8 +19,9 @@
 CL = 8
 SEQ = 16
 OWN = 4
-CH = 4
-ROWS = BLK // CH
+ROWS = (16, 16, 32, 32, 32)
+CH = len(ROWS)
+FIRST = tuple(sum(ROWS[:c]) for c in range(CH))
 GROUPS = 4
 WCOL = 3 * D // GROUPS
 SIDE = 8
@@ -37,54 +38,19 @@
     return pltpu.roll(x, HD, x.ndim - 1)
 
 
-def body(
-    ids_s,
-    cnt_s,
-    nodes,
-    ids_v,
-    w_hbm,
-    o_ref,
-    w_v,
-    kvs,
-    kvc0,
-    kvc1,
-    kvc2,
-    kvc3,
-    qs,
-    qr,
-    snd,
-    far0,
-    far1,
-    far2,
-    far3,
-    lsend,
-    lrecv,
-    lsm,
-    far_v,
-    far_s,
-    sc,
-    acc_v,
-    top_v,
-    outs,
-    ret,
-    w_sem,
-    l_ss,
-    l_rs,
-    kv_ss,
-    kv_rs,
-    q_ss,
-    q_rs,
-    z_ss,
-    z_rs,
-    r_ss,
-    r_rs,
-    own_sem,
-    sm_sem,
-):
+def body(ids_s, cnt_s, nodes, ids_v, w_hbm, wo_hbm, o_ref, *scratch):
     me = lax.axis_index("seq")
     mc = lax.axis_index("cluster")
-    kvc = (kvc0, kvc1, kvc2, kvc3)
-    far = (far0, far1, far2, far3)
+    scratch = list(scratch)
+
+    def take(n):
+        got = scratch[:n]
+        del scratch[:n]
+        return got
+
+    kvs, kvc, snd, far = take(CH), take(CH), take(CH), take(CH)
+    w_v, wo_v, qs, qr, lsend, lrecv, lsm, far_v, far_s, sc, acc_v, top_v, outs, ret, att = take(15)
+    w_sem, l_ss, l_rs, kv_ss, kv_rs, q_ss, q_rs, z_ss, z_rs, r_ss, r_rs, own_sem, sm_sem = scratch
 
     barrier = pltpu.get_barrier_semaphore()
 
@@ -96,40 +62,23 @@
     def _(d):
         pl.semaphore_signal(barrier, inc=1, device_id={"cluster": lax.rem(mc + d, CL)}, device_id_type=MESH)
 
-    def w_copy(g):
+    def w_copy(k):
+        g = lax.rem(me // GROUPS + k, GROUPS)
         return pltpu.make_async_copy(
-            w_hbm.at[:, pl.ds(pl.multiple_of(g * WCOL, 128), WCOL)], w_v.at[g], w_sem.at[g]
+            w_hbm.at[:, pl.ds(pl.multiple_of(g * WCOL, 128), WCOL)], w_v.at[k], w_sem.at[k]
         )
 
     @pl.loop(0, GROUPS)
-    def _(g):
-        w_copy(g).start()
-
-    @pl.loop(0, GROUPS)
-    def _(g):
-        w_copy(g).wait()
-        p = jnp.dot(nodes[...], w_v[g], preferred_element_type=F32)
-        low = low_lanes((OWN * BLK, 128))
-        half = OWN * BLK // 2
-        scale = HD**-0.5
-        for k in range(2):
-            t0, t1, t2 = (p[:, 384 * k + 128 * n : 384 * k + 128 * n + 128] for n in range(3))
-            r0, r1 = swap_halves(t0), swap_halves(t1)
-            h0 = 4 * g + 2 * k
-            kv0 = jnp.where(low, r0, r1).astype(BF16).reshape(OWN, BLK, 128)
-            kv1 = t2.astype(BF16).reshape(OWN, BLK, 128)
-            for c in range(CH):
-                kvs[h0, c] = kv0[:, c * ROWS : (c + 1) * ROWS]
-                kvs[h0 + 1, c] = kv1[:, c * ROWS : (c + 1) * ROWS]
-            q0 = jnp.where(low[:half], t0[:half], r0[half:]) * scale
-            q1 = jnp.where(low[:half], r1[:half], t1[half:]) * scale
-            qs[h0] = q0.astype(BF16).reshape(2, BLK, 128)
-            qs[h0 + 1] = q1.astype(BF16).reshape(2, BLK, 128)
+    def _(k):
+        w_copy(k).start()
+
+    wo_copy = pltpu.make_async_copy(wo_hbm, wo_v, w_sem.at[GROUPS])
+    wo_copy.start()
 
     def kv_copy(c, d):
         peer = lax.rem(me + d, SEQ)
         return pltpu.make_async_remote_copy(
-            src_ref=kvs.at[peer, c],
+            src_ref=kvs[c].at[peer],
             dst_ref=kvc[c].at[pl.ds(OWN * me, OWN)],
             send_sem=kv_ss.at[c, d],
             recv_sem=kv_rs.at[c, d],
@@ -138,7 +87,7 @@
         )
 
     def kv_own(c):
-        return pltpu.make_async_copy(kvs.at[me, c], kvc[c].at[pl.ds(OWN * me, OWN)], own_sem.at[c])
+        return pltpu.make_async_copy(kvs[c].at[me], kvc[c].at[pl.ds(OWN * me, OWN)], own_sem.at[c])
 
     def q_copy(i, d):
         peer = lax.rem(me + d, SEQ)
@@ -167,7 +116,7 @@
 
     def z_copy(c, d):
         return pltpu.make_async_remote_copy(
-            src_ref=snd.at[c, d],
+            src_ref=snd[c].at[d],
             dst_ref=far[c].at[pl.ds(REQ * mc, REQ)],
             send_sem=z_ss.at[c, d],
             recv_sem=z_rs.at[c, d],
@@ -220,11 +169,8 @@
         @pl.loop(1, CL)
         def _(d):
             for r in range(REQ):
-                snd[c, d, r] = kvc[c][lsm[d, r, 0] & (QB - 1)]
+                snd[c][d, r] = kvc[c][lsm[d, 0, r] & (QB - 1)]
             z_copy(c, d).start()
-
-    pl.semaphore_wait(barrier, SEQ + CL - 2)
-    start(kv_own(0), kv(0))
 
     lane = lax.broadcasted_iota(jnp.int32, (QB, CL * QB), 1)
     hits = [ids_v[:, NEAR + j : NEAR + j + 1] == lane for j in range(REMOTE)]
@@ -239,26 +185,65 @@
         rank = rank + jnp.where(inner >= step, pltpu.roll(rank, step, 1), 0.0)
         step *= 2
     rank = rank - present
+    slot = lax.broadcasted_iota(jnp.int32, (REQ, CL * QB), 0).astype(F32)
+    wanted = jnp.where((slot == rank[:1]) & (present[:1] > 0.5), 1.0, 0.0).astype(BF16)
+    sub8 = lax.broadcasted_iota(jnp.int32, (CL, CL * QB), 0)
+    worth = jnp.where(lane8 // QB == sub8, inner, 0).astype(F32).astype(BF16)
+    wanted = jnp.concatenate([wanted, jnp.zeros((128 - REQ, CL * QB), BF16)], axis=0)
+    lists = lax.dot_general(
+        worth, wanted, (((1,), (1,)), ((), ())), preferred_element_type=F32
+    ).astype(jnp.int32)
+    for p in range(CL):
+        lsend[p] = lists[p : p + 1]
     place = rank + (lane8 // QB * REQ).astype(F32)
+    lane_q = lax.broadcasted_iota(jnp.int32, (QB, 128), 1)
+    table = jnp.zeros((QB, 128), F32)
     for j in range(REMOTE):
         at = jnp.sum(jnp.where(hits[j], place[:1], 0.0), axis=1, keepdims=True)
-        far_v[j] = jnp.broadcast_to(at, (QB, 128)).astype(jnp.int32)
-    slot = lax.broadcasted_iota(jnp.int32, (REQ, CL * QB), 0).astype(F32)
-    wanted = jnp.where((slot == rank[:1]) & (present[:1] > 0.5), inner[:1].astype(F32), 0.0)
-    lane_r = lax.broadcasted_iota(jnp.int32, (REQ, 128), 1)
-    for p in range(CL):
-        tile = wanted[:, p // 2 * 128 : p // 2 * 128 + 128]
-        mine = jnp.where((lane_r >= HD) == (p % 2 == 1), tile, 0.0)
-        block = jnp.sum(mine, axis=1, keepdims=True)
-        lsend[p] = jnp.broadcast_to(block, (REQ, 128)).astype(jnp.int32)
-
-    @pl.loop(1, CL)
-    def _(d):
-        list_copy(d).start()
-
+        table = jnp.where(lane_q == j, at, table)
+    far_v[...] = table.astype(jnp.int32)
     far_copy = pltpu.make_async_copy(far_v, far_s, sm_sem.at[1])
     far_copy.start()
 
+    @pl.loop(0, GROUPS)
+    def _(k):
+        g = lax.rem(me // GROUPS + k, GROUPS)
+        w_copy(k).wait()
+        p = jnp.dot(nodes[...], w_v[k], preferred_element_type=F32)
+        low = low_lanes((OWN * BLK, 128))
+        half = OWN * BLK // 2
+        scale = HD**-0.5
+        for n in range(2):
+            t0, t1, t2 = (p[:, 384 * n + 128 * e : 384 * n + 128 * e + 128] for e in range(3))
+            r0, r1 = swap_halves(t0), swap_halves(t1)
+            h0 = 4 * g + 2 * n
+            kv0 = jnp.where(low, r0, r1).astype(BF16).reshape(OWN, BLK, 128)
+            kv1 = t2.astype(BF16).reshape(OWN, BLK, 128)
+            for c in range(CH):
+                kvs[c][h0] = kv0[:, FIRST[c] : FIRST[c] + ROWS[c]]
+                kvs[c][h0 + 1] = kv1[:, FIRST[c] : FIRST[c] + ROWS[c]]
+            q0 = jnp.where(low[:half], t0[:half], r0[half:]) * scale
+            q1 = jnp.where(low[:half], r1[:half], t1[half:]) * scale
+            qs[h0] = q0.astype(BF16).reshape(2, BLK, 128)
+            qs[h0 + 1] = q1.astype(BF16).reshape(2, BLK, 128)
+
+        @pl.when(k == 0)
+        def _():
+            pl.semaphore_wait(barrier, SEQ + CL - 2)
+
+            @pl.loop(1, CL)
+            def _(d):
+                list_copy(d).start()
+
+        @pl.loop(0, HEADS // GROUPS)
+        def _(h):
+            d = lax.rem(g * (HEADS // GROUPS) + h + SEQ - me, SEQ)
+
+            @pl.when(d > 0)
+            def _():
+                kv_copy(0, d).start()
+
+    kv_own(0).start()
     start_after(kv(0), kv_own(1), kv(1))
 
     @pl.loop(1, CL)
@@ -270,19 +255,14 @@
     )
     sm_copy.start()
     sm_copy.wait()
-    far_copy.wait()
-
-    landed(kv_own(0), kv(0))
-    pack(0)
-    start_after(kv(1), kv_own(2), kv(2))
-    landed(kv_own(1), kv(1))
-    pack(1)
-    start_after(kv(2), kv_own(3), kv(3))
-    landed(kv_own(2), kv(2))
-    pack(2)
-    start_after(kv(3), q_own(0), qq(0))
-    landed(kv_own(3), kv(3))
-    pack(3)
+
+    for c in range(CH):
+        landed(kv_own(c), kv(c))
+        pack(c)
+        if c + 2 < CH:
+            start_after(kv(c + 1), kv_own(c + 2), kv(c + 2))
+        elif c + 2 == CH:
+            start_after(kv(c + 1), q_own(0), qq(0))
     start_after(qq(0), q_own(1), qq(1))
 
     def block_of(bufs, b):
@@ -296,7 +276,7 @@
 
     def far_pair(qb, j):
         last = CL * REQ - 1
-        return pair_of(far, far_s[j, qb, 0] & last, far_s[j + 1, qb, 0] & last)
+        return pair_of(far, far_s[qb, j] & last, far_s[qb, j + 1] & last)
 
     def score(q, kv):
         return lax.dot_general(q, kv, (((1,), (1,)), ((), ())), preferred_element_type=F32)
@@ -395,6 +375,7 @@
         def _(d, c=c):
             z_copy(c, d).wait()
 
+    far_copy.wait()
     for i in range(2):
         distant(i)
         ret_own(i).start()
@@ -403,6 +384,7 @@
     def _(d):
         q_copy(1, d).wait_send()
 
+    wo_copy.wait()
     for i in range(2):
         ret_own(i).wait()
 
@@ -410,43 +392,49 @@
         def _(d, i=i):
             ret_copy(i, lax.rem(me + d, SEQ), d).wait()
 
-    for g in range(HEADS // 2):
-        for i in range(2):
+        for g in range(HEADS // 2):
             a = ret[i, 2 * g].astype(F32)
             b = ret[i, 2 * g + 1].astype(F32)
             low = low_lanes(a.shape)
-            o_ref[i, :, g * 128 : (g + 1) * 128] = jnp.where(low, a, swap_halves(b)).astype(BF16)
-            o_ref[2 + i, :, g * 128 : (g + 1) * 128] = jnp.where(low, swap_halves(a), b).astype(BF16)
+            col = slice(g * 128, (g + 1) * 128)
+            att[:BLK, col] = jnp.where(low, a, swap_halves(b)).astype(BF16)
+            att[BLK:, col] = jnp.where(low, swap_halves(a), b).astype(BF16)
+        out = jnp.dot(att[...], wo_v[...], preferred_element_type=F32).astype(BF16)
+        o_ref[i] = out[:BLK]
+        o_ref[2 + i] = out[BLK:]
 
 
 def on_device(nodes, w_qkv, w_out, kv_ids, counts):
     vm = pl.BlockSpec(memory_space=pltpu.VMEM)
     sm = pl.BlockSpec(memory_space=pltpu.SMEM)
+    hbm = pl.BlockSpec(memory_space=pl.ANY)
     dma = pltpu.SemaphoreType.DMA
-    attended = pl.pallas_call(
+    out = pl.pallas_call(
         body,
         out_shape=jax.ShapeDtypeStruct((OWN, BLK, D), BF16),
-        in_specs=[sm, sm, vm, vm, pl.BlockSpec(memory_space=pl.ANY)],
+        in_specs=[sm, sm, vm, vm, hbm, hbm],
         out_specs=vm,
         scratch_shapes=[
+            *[pltpu.VMEM((HEADS, OWN, r, 128), BF16) for r in ROWS],
+            *[pltpu.VMEM((QB, r, 128), BF16) for r in ROWS],
+            *[pltpu.VMEM((CL, REQ, r, 128), BF16) for r in ROWS],
+            *[pltpu.VMEM((CL * REQ, r, 128), BF16) for r in ROWS],
             pltpu.VMEM((GROUPS, D, WCOL), BF16),
-            pltpu.VMEM((HEADS, CH, OWN, ROWS, 128), BF16),
-            *[pltpu.VMEM((QB, ROWS, 128), BF16) for _ in range(CH)],
+            pltpu.VMEM((D, D), BF16),
             pltpu.VMEM((HEADS, 2, BLK, 128), BF16),
             pltpu.VMEM((2, SEQ, BLK, 128), BF16),
-            pltpu.VMEM((CH, CL, REQ, ROWS, 128), BF16),
-            *[pltpu.VMEM((CL * REQ, ROWS, 128), BF16) for _ in range(CH)],
-            pltpu.VMEM((CL, REQ, 128), jnp.int32),
-            pltpu.VMEM((CL, REQ, 128), jnp.int32),
-            pltpu.SMEM((CL, REQ, 128), jnp.int32),
-            pltpu.VMEM((REMOTE, QB, 128), jnp.int32),
-            pltpu.SMEM((REMOTE, QB, 128), jnp.int32),
+            pltpu.VMEM((CL, 1, 128), jnp.int32),
+            pltpu.VMEM((CL, 1, 128), jnp.int32),
+            pltpu.SMEM((CL, 1, 128), jnp.int32),
+            pltpu.VMEM((QB, 128), jnp.int32),
+            pltpu.SMEM((QB, 128), jnp.int32),
             pltpu.VMEM((SIDE, NEAR // 2, BLK, 2 * BLK), F32),
             pltpu.VMEM((2, SEQ, 2, BLK, 128), F32),
             pltpu.VMEM((2, SEQ, 2, BLK, 128), F32),
             pltpu.VMEM((2, SEQ, BLK, 128), BF16),
             pltpu.VMEM((2, SEQ, BLK, 128), BF16),
-            dma((GROUPS,)),
+            pltpu.VMEM((2 * BLK, D), BF16),
+            dma((GROUPS + 1,)),
             dma((CL,)),
             dma((CL,)),
             dma((CH, SEQ)),
@@ -464,8 +452,8 @@
             collective_id=0, has_side_effects=True, vmem_limit_bytes=60 << 20
         ),
         name="sublayer",
-    )(kv_ids, counts, nodes, kv_ids, w_qkv)
-    return jnp.dot(attended.reshape(OWN * BLK, D), w_out, preferred_element_type=F32).astype(BF16)
+    )(kv_ids, counts, nodes, kv_ids, w_qkv, w_out)
+    return out.reshape(OWN * BLK, D)
 
 
 def solution(mesh):

time: 95.8 us -> 90.8 us (0.948)
  matrix products: 3.45 us -> 0 us
  Pallas kernels: 90.1 us -> 86.9 us
  local copies, waits for them, and re-layouts: 1.55 us -> 3.66 us
    dot_general x1 -> x0, matrix products: 3.45 us -> none  [on_device(): jnp.dot(attended.reshape(OWN * BLK, D), w_out, preferred_element_type=F32)]
    pallas_call x1, Pallas kernels: 90.1 us -> 86.9 us  [on_device(): pl.pallas_call(body, out_shape=jax.ShapeDtypeStruct((OWN, BLK, D), BF16),...]
    unnamed x3 -> x2, local copies, waits for them, and re-layouts: 1.55 us -> 3.66 us
where the time goes in v3:
time: 90.8 us; the launch traced here: 90.6 us
  Pallas kernels  86.9 us (96%)
  local copies, waits for them, and re-layouts  3.66 us (4%)
    pallas_call x1, Pallas kernels, on_device(): pl.pallas_call(body, out_shape=jax.ShapeDtypeStruct((OWN, BLK, D), BF16),...  86.9 us
    unnamed x2, local copies, waits for them, and re-layouts  3.66 us

profile of v3, /device:TPU:1, one launch (start us, length us, event | category | flops | bytes accessed | tf_op | source)
XLA Modules:
  0.0 90.6 jit_solution(4024301122872952336)
XLA Ops:
  0.0 1.4 %copy.6.ids_s.ids_v = s32[64,16]{1,0:T(8,128)} copy(s32[64,16]{0,1:T(8,128)} %param.8) | data formatting | bytes 8192 | tf_op args[3]
  1.4 86.9 %sublayer.1 = bf16[4,128,1024]{2,1,0:T(8,128)(2,1)} custom-call(s32[64,16]{1,0:T(8,128)} %copy.6.ids_s.ids_v, s32[64]{0:T(128)} %cnt_s.1, bf16[512,1024]{1,0:T(8,128)(2,1)} %nodes.1, s32[64,16]{1,0:T(8,128)} %copy.6.ids_s.ids_v, bf16[1024,3072]{1,0:T(8,128)(2,1)} %w_hbm.1, bf16[1024,1024]{1,0:T(8,128)(2,1)} %wo_hbm.1), custom_call_target="tpu_custom_call" | custom-call | tf_op jit(solution)/shard_map/sublayer/pallas_call | solution.py:412
  88.3 2.3 %copy.9 = bf16[512,1024]{1,0:T(8,128)(2,1)} copy(bf16[512,1024]{1,0:T(8,128)(2,1)} %bitcast.1) | data formatting | bytes 2097152

commit v4 on v3

--- a/solution.py
+++ b/solution.py
@@ -49,7 +49,7 @@
         return got
 
     kvs, kvc, snd, far = take(CH), take(CH), take(CH), take(CH)
-    w_v, wo_v, qs, qr, lsend, lrecv, lsm, far_v, far_s, sc, acc_v, top_v, outs, ret, att = take(15)
+    w_v, wo_v, qs, qr, lsend, lrecv, lsm, far_v, far_s, sc, acc_v, top_v, outs, ret, att, turn = take(16)
     w_sem, l_ss, l_rs, kv_ss, kv_rs, q_ss, q_rs, z_ss, z_rs, r_ss, r_rs, own_sem, sm_sem = scratch
 
     barrier = pltpu.get_barrier_semaphore()
@@ -172,8 +172,11 @@
                 snd[c][d, r] = kvc[c][lsm[d, 0, r] & (QB - 1)]
             z_copy(c, d).start()
 
-    lane = lax.broadcasted_iota(jnp.int32, (QB, CL * QB), 1)
-    hits = [ids_v[:, NEAR + j : NEAR + j + 1] == lane for j in range(REMOTE)]
+    turn[...] = jnp.zeros((128, 128), F32)
+    turn[:KVB, :QB] = ids_v[...].astype(F32)
+    ids_t = jnp.transpose(turn[...])
+    lane = lax.broadcasted_iota(jnp.int32, (QB, CL * QB), 1).astype(F32)
+    hits = [ids_t[:QB, NEAR + j : NEAR + j + 1] == lane for j in range(REMOTE)]
     named = jnp.where(hits[0] | hits[1] | hits[2] | hits[3], 1.0, 0.0)
     present = jnp.max(named, axis=0, keepdims=True)
     present = jnp.broadcast_to(present, (8, CL * QB))
@@ -205,58 +208,84 @@
     far_copy = pltpu.make_async_copy(far_v, far_s, sm_sem.at[1])
     far_copy.start()
 
+    def project(k, x):
+        p = jnp.dot(x, w_v[k], preferred_element_type=F32)
+        return [[p[:, 384 * n + 128 * e : 384 * n + 128 * e + 128] for e in range(3)] for n in range(2)]
+
+    def group(k):
+        return lax.rem(me // GROUPS + k, GROUPS)
+
+    def send_group(c, k):
+        @pl.loop(0, HEADS // GROUPS)
+        def _(h):
+            d = lax.rem(group(k) * (HEADS // GROUPS) + h + SEQ - me, SEQ)
+
+            @pl.when(d > 0)
+            def _():
+                kv_copy(c, d).start()
+
+    x0 = jnp.concatenate([nodes[b * BLK : b * BLK + ROWS[0]] for b in range(OWN)], axis=0)
+
     @pl.loop(0, GROUPS)
     def _(k):
-        g = lax.rem(me // GROUPS + k, GROUPS)
         w_copy(k).wait()
-        p = jnp.dot(nodes[...], w_v[k], preferred_element_type=F32)
+        low = low_lanes((OWN * ROWS[0], 128))
+        for n, (t0, t1, t2) in enumerate(project(k, x0)):
+            h0 = 4 * group(k) + 2 * n
+            kv0 = jnp.where(low, swap_halves(t0), swap_halves(t1))
+            kvs[0][h0] = kv0.astype(BF16).reshape(OWN, ROWS[0], 128)
+            kvs[0][h0 + 1] = t2.astype(BF16).reshape(OWN, ROWS[0], 128)
+
+        @pl.when(k == 0)
+        def _():
+            pl.semaphore_wait(barrier, SEQ + CL - 2)
+
+            @pl.loop(1, CL)
+            def _(d):
+                list_copy(d).start()
+
+        send_group(0, k)
+
+    kv_own(0).start()
+
+    @pl.loop(0, GROUPS)
+    def _(k):
+        @pl.when(k == GROUPS // 2)
+        def _():
+            @pl.loop(1, CL)
+            def _(d):
+                list_copy(d).wait()
+
+            sm_copy = pltpu.make_async_copy(
+                lrecv.at[pl.ds(1, CL - 1)], lsm.at[pl.ds(1, CL - 1)], sm_sem.at[0]
+            )
+            sm_copy.start()
+            sm_copy.wait()
+
+
+            landed(kv_own(0), kv(0))
+            pack(0)
+
         low = low_lanes((OWN * BLK, 128))
         half = OWN * BLK // 2
         scale = HD**-0.5
-        for n in range(2):
-            t0, t1, t2 = (p[:, 384 * n + 128 * e : 384 * n + 128 * e + 128] for e in range(3))
+        for n, (t0, t1, t2) in enumerate(project(k, nodes[...])):
             r0, r1 = swap_halves(t0), swap_halves(t1)
-            h0 = 4 * g + 2 * n
+            h0 = 4 * group(k) + 2 * n
             kv0 = jnp.where(low, r0, r1).astype(BF16).reshape(OWN, BLK, 128)
             kv1 = t2.astype(BF16).reshape(OWN, BLK, 128)
-            for c in range(CH):
+            for c in range(1, CH):
                 kvs[c][h0] = kv0[:, FIRST[c] : FIRST[c] + ROWS[c]]
                 kvs[c][h0 + 1] = kv1[:, FIRST[c] : FIRST[c] + ROWS[c]]
             q0 = jnp.where(low[:half], t0[:half], r0[half:]) * scale
             q1 = jnp.where(low[:half], r1[:half], t1[half:]) * scale
             qs[h0] = q0.astype(BF16).reshape(2, BLK, 128)
             qs[h0 + 1] = q1.astype(BF16).reshape(2, BLK, 128)
-
-        @pl.when(k == 0)
-        def _():
-            pl.semaphore_wait(barrier, SEQ + CL - 2)
-
-            @pl.loop(1, CL)
-            def _(d):
-                list_copy(d).start()
-
-        @pl.loop(0, HEADS // GROUPS)
-        def _(h):
-            d = lax.rem(g * (HEADS // GROUPS) + h + SEQ - me, SEQ)
-
-            @pl.when(d > 0)
-            def _():
-                kv_copy(0, d).start()
-
-    kv_own(0).start()
-    start_after(kv(0), kv_own(1), kv(1))
-
-    @pl.loop(1, CL)
-    def _(d):
-        list_copy(d).wait()
-
-    sm_copy = pltpu.make_async_copy(
-        lrecv.at[pl.ds(1, CL - 1)], lsm.at[pl.ds(1, CL - 1)], sm_sem.at[0]
-    )
-    sm_copy.start()
-    sm_copy.wait()
-
-    for c in range(CH):
+        send_group(1, k)
+
+    kv_own(1).start()
+    start_after(kv(1), kv_own(2), kv(2))
+    for c in range(1, CH):
         landed(kv_own(c), kv(c))
         pack(c)
         if c + 2 < CH:
@@ -272,7 +301,7 @@
         return jnp.concatenate(block_of(bufs, b0) + block_of(bufs, b1), axis=0)
 
     def near_pair(qb, j):
-        return pair_of(kvc, ids_s[qb, j] & (QB - 1), ids_s[qb, j + 1] & (QB - 1))
+        return pair_of(kvc, ids_s[j, qb] & (QB - 1), ids_s[j + 1, qb] & (QB - 1))
 
     def far_pair(qb, j):
         last = CL * REQ - 1
@@ -383,6 +412,7 @@
     @pl.loop(1, SEQ)
     def _(d):
         q_copy(1, d).wait_send()
+        kv_copy(0, d).wait_send()
 
     wo_copy.wait()
     for i in range(2):
@@ -404,6 +434,14 @@
         o_ref[2 + i] = out[BLK:]
 
 
+def write_out(x_ref, o_ref, sem):
+    copies = [pltpu.make_async_copy(x_ref.at[b], o_ref.at[b], sem.at[b]) for b in range(OWN)]
+    for copy in copies:
+        copy.start()
+    for copy in copies:
+        copy.wait()
+
+
 def on_device(nodes, w_qkv, w_out, kv_ids, counts):
     vm = pl.BlockSpec(memory_space=pltpu.VMEM)
     sm = pl.BlockSpec(memory_space=pltpu.SMEM)
@@ -411,7 +449,7 @@
     dma = pltpu.SemaphoreType.DMA
     out = pl.pallas_call(
         body,
-        out_shape=jax.ShapeDtypeStruct((OWN, BLK, D), BF16),
+        out_shape=pltpu.VMEM((OWN, BLK, D), BF16),
         in_specs=[sm, sm, vm, vm, hbm, hbm],
         out_specs=vm,
         scratch_shapes=[
@@ -434,6 +472,7 @@
             pltpu.VMEM((2, SEQ, BLK, 128), BF16),
             pltpu.VMEM((2, SEQ, BLK, 128), BF16),
             pltpu.VMEM((2 * BLK, D), BF16),
+            pltpu.VMEM((128, 128), F32),
             dma((GROUPS + 1,)),
             dma((CL,)),
             dma((CL,)),
@@ -452,8 +491,16 @@
             collective_id=0, has_side_effects=True, vmem_limit_bytes=60 << 20
         ),
         name="sublayer",
-    )(kv_ids, counts, nodes, kv_ids, w_qkv, w_out)
-    return out.reshape(OWN * BLK, D)
+    )(kv_ids.T, counts, nodes, kv_ids.T, w_qkv, w_out)
+    return pl.pallas_call(
+        write_out,
+        out_shape=jax.ShapeDtypeStruct((OWN, BLK, D), BF16),
+        in_specs=[vm],
+        out_specs=hbm,
+        scratch_shapes=[dma((OWN,))],
+        compiler_params=pltpu.CompilerParams(vmem_limit_bytes=1 << 20),
+        name="write_out",
+    )(out).reshape(OWN * BLK, D)
 
 
 def solution(mesh):

time: 90.8 us -> 88.1 us (0.970)
  local copies, waits for them, and re-layouts: 3.66 us -> 0 us
    unnamed x2 -> x0, local copies, waits for them, and re-layouts: 3.66 us -> none
    pallas_call x1 -> x2, Pallas kernels: 86.9 us -> 87.6 us  [the longest x1 86.6 us: on_device(): pl.pallas_call(body, out_shape=pltpu.VMEM((OWN, BLK, D), BF16), in_specs=...]
where the time goes in v4:
time: 88.1 us; the launch traced here: 87.6 us
  Pallas kernels  87.6 us (99%)
    pallas_call x1, Pallas kernels, on_device(): pl.pallas_call(body, out_shape=pltpu.VMEM((OWN, BLK, D), BF16), in_specs=...  86.6 us

profile of v4, /device:TPU:1, one launch (start us, length us, event | category | flops | bytes accessed | tf_op | source)
XLA Modules:
  0.0 87.6 jit_solution(2199158598203964905)
XLA Ops:
  0.0 86.6 %sublayer.1.x_ref = bf16[4,128,1024]{2,1,0:T(8,128)(2,1)S(1)} custom-call(s32[16,64]{1,0:T(8,128)} %bitcast.2, s32[64]{0:T(128)} %cnt_s.1, bf16[512,1024]{1,0:T(8,128)(2,1)} %nodes.1, s32[16,64]{1,0:T(8,128)} %bitcast.3, bf16[1024,3072]{1,0:T(8,128)(2,1)} %w_hbm.1, bf16[1024,1024]{1,0:T(8,128)(2,1)} %wo_hbm.1), custom_call_target="tpu_custom_call" | custom-call | tf_op jit(solution)/shard_map/sublayer/pallas_call | solution.py:450
  86.6 1.0 %write_out.1 = bf16[4,128,1024]{2,1,0:T(8,128)(2,1)} custom-call(bf16[4,128,1024]{2,1,0:T(8,128)(2,1)S(1)} %sublayer.1.x_ref), custom_call_target="tpu_custom_call" | custom-call | tf_op jit(solution)/shard_map/write_out/pallas_call | solution.py:495

commit v5 on v4

--- a/solution.py
+++ b/solution.py
@@ -14,17 +14,19 @@
 KVB = 16
 REMOTE = 4
 NEAR = KVB - REMOTE
+LEAST = 13
 QB = 64
 REQ = 16
 CL = 8
 SEQ = 16
 OWN = 4
-ROWS = (16, 16, 32, 32, 32)
+ROWS = (32, 32, 32, 32)
 CH = len(ROWS)
 FIRST = tuple(sum(ROWS[:c]) for c in range(CH))
 GROUPS = 4
 WCOL = 3 * D // GROUPS
 SIDE = 8
+WIDE = 16
 MESH = pl.DeviceIdType.MESH
 F32 = jnp.float32
 BF16 = jnp.bfloat16
@@ -38,7 +40,7 @@
     return pltpu.roll(x, HD, x.ndim - 1)
 
 
-def body(ids_s, cnt_s, nodes, ids_v, w_hbm, wo_hbm, o_ref, *scratch):
+def body(ids_s, cnt_s, nodes_hbm, ids_hbm, w_hbm, wo_hbm, o_ref, *scratch):
     me = lax.axis_index("seq")
     mc = lax.axis_index("cluster")
     scratch = list(scratch)
@@ -49,18 +51,20 @@
         return got
 
     kvs, kvc, snd, far = take(CH), take(CH), take(CH), take(CH)
-    w_v, wo_v, qs, qr, lsend, lrecv, lsm, far_v, far_s, sc, acc_v, top_v, outs, ret, att, turn = take(16)
+    w_v, wo_v, qs, qr, lsend, lrecv, lsm, far_v, far_s, sc, acc_v, top_v, outs, ret, att, turn, nodes, ids_v = take(18)
     w_sem, l_ss, l_rs, kv_ss, kv_rs, q_ss, q_rs, z_ss, z_rs, r_ss, r_rs, own_sem, sm_sem = scratch
 
     barrier = pltpu.get_barrier_semaphore()
 
-    @pl.loop(1, SEQ)
-    def _(d):
+    for d in range(1, SEQ):
         pl.semaphore_signal(barrier, inc=1, device_id={"seq": lax.rem(me + d, SEQ)}, device_id_type=MESH)
-
-    @pl.loop(1, CL)
-    def _(d):
+    for d in range(1, CL):
         pl.semaphore_signal(barrier, inc=1, device_id={"cluster": lax.rem(mc + d, CL)}, device_id_type=MESH)
+
+    ids_copy = pltpu.make_async_copy(ids_hbm, ids_v, sm_sem.at[2])
+    ids_copy.start()
+    nodes_copy = pltpu.make_async_copy(nodes_hbm, nodes, sm_sem.at[3])
+    nodes_copy.start()
 
     def w_copy(k):
         g = lax.rem(me // GROUPS + k, GROUPS)
@@ -73,8 +77,6 @@
         w_copy(k).start()
 
     wo_copy = pltpu.make_async_copy(wo_hbm, wo_v, w_sem.at[GROUPS])
-    wo_copy.start()
-
     def kv_copy(c, d):
         peer = lax.rem(me + d, SEQ)
         return pltpu.make_async_remote_copy(
@@ -173,6 +175,7 @@
             z_copy(c, d).start()
 
     turn[...] = jnp.zeros((128, 128), F32)
+    ids_copy.wait()
     turn[:KVB, :QB] = ids_v[...].astype(F32)
     ids_t = jnp.transpose(turn[...])
     lane = lax.broadcasted_iota(jnp.int32, (QB, CL * QB), 1).astype(F32)
@@ -215,15 +218,7 @@
     def group(k):
         return lax.rem(me // GROUPS + k, GROUPS)
 
-    def send_group(c, k):
-        @pl.loop(0, HEADS // GROUPS)
-        def _(h):
-            d = lax.rem(group(k) * (HEADS // GROUPS) + h + SEQ - me, SEQ)
-
-            @pl.when(d > 0)
-            def _():
-                kv_copy(c, d).start()
-
+    nodes_copy.wait()
     x0 = jnp.concatenate([nodes[b * BLK : b * BLK + ROWS[0]] for b in range(OWN)], axis=0)
 
     @pl.loop(0, GROUPS)
@@ -236,36 +231,16 @@
             kvs[0][h0] = kv0.astype(BF16).reshape(OWN, ROWS[0], 128)
             kvs[0][h0 + 1] = t2.astype(BF16).reshape(OWN, ROWS[0], 128)
 
-        @pl.when(k == 0)
-        def _():
-            pl.semaphore_wait(barrier, SEQ + CL - 2)
-
-            @pl.loop(1, CL)
-            def _(d):
-                list_copy(d).start()
-
-        send_group(0, k)
-
+    pl.semaphore_wait(barrier, SEQ + CL - 2)
+    for d in range(1, CL):
+        list_copy(d).start()
+    for d in range(1, SEQ):
+        kv_copy(0, d).start()
     kv_own(0).start()
+    wo_copy.start()
 
     @pl.loop(0, GROUPS)
     def _(k):
-        @pl.when(k == GROUPS // 2)
-        def _():
-            @pl.loop(1, CL)
-            def _(d):
-                list_copy(d).wait()
-
-            sm_copy = pltpu.make_async_copy(
-                lrecv.at[pl.ds(1, CL - 1)], lsm.at[pl.ds(1, CL - 1)], sm_sem.at[0]
-            )
-            sm_copy.start()
-            sm_copy.wait()
-
-
-            landed(kv_own(0), kv(0))
-            pack(0)
-
         low = low_lanes((OWN * BLK, 128))
         half = OWN * BLK // 2
         scale = HD**-0.5
@@ -281,11 +256,19 @@
             q1 = jnp.where(low[:half], r1[:half], t1[half:]) * scale
             qs[h0] = q0.astype(BF16).reshape(2, BLK, 128)
             qs[h0 + 1] = q1.astype(BF16).reshape(2, BLK, 128)
-        send_group(1, k)
-
-    kv_own(1).start()
-    start_after(kv(1), kv_own(2), kv(2))
-    for c in range(1, CH):
+
+    start_after(kv(0), kv_own(1), kv(1))
+    @pl.loop(1, CL)
+    def _(d):
+        list_copy(d).wait()
+
+    sm_copy = pltpu.make_async_copy(
+        lrecv.at[pl.ds(1, CL - 1)], lsm.at[pl.ds(1, CL - 1)], sm_sem.at[0]
+    )
+    sm_copy.start()
+    sm_copy.wait()
+
+    for c in range(CH):
         landed(kv_own(c), kv(c))
         pack(c)
         if c + 2 < CH:
@@ -322,19 +305,19 @@
         right = jnp.where(low, swap_halves(qp.astype(F32)), 0.0).astype(BF16)
         return left, right
 
-    def items_of(i, first):
+    def items_of(i, first, count):
         items = []
-        for u in range(SIDE // 2):
+        for u in range(count // 2):
             s = lax.rem(me + first + u, SEQ)
             for half, q in enumerate(queries(i, s)):
                 items.append((s, half, q, s * OWN + i + 2 * half))
         return items
 
     def near(i):
-        @pl.loop(0, 2 * SEQ // SIDE)
+        @pl.loop(0, 2 * SEQ // WIDE)
         def _(t):
-            items = items_of(i, t * (SIDE // 2))
-            tops = [None] * SIDE
+            items = items_of(i, t * (WIDE // 2), WIDE)
+            tops = [None] * WIDE
             for jj in range(NEAR // 2):
                 for g, (s, half, q, qb) in enumerate(items):
                     sco = score(q, near_pair(qb, 2 * jj))
@@ -342,7 +325,7 @@
                     top = jnp.maximum(sco[:, :BLK], sco[:, BLK:])
                     tops[g] = top if jj == 0 else jnp.maximum(tops[g], top)
             tops = [jnp.max(top, axis=1, keepdims=True) for top in tops]
-            accs = [None] * SIDE
+            accs = [None] * WIDE
             for jj in range(NEAR // 2):
                 for g, (s, half, q, qb) in enumerate(items):
                     a = weigh(sc[g, jj], tops[g], near_pair(qb, 2 * jj))
@@ -354,7 +337,7 @@
     def distant(i):
         @pl.loop(0, 2 * SEQ // SIDE)
         def _(t):
-            items = items_of(i, t * (SIDE // 2))
+            items = items_of(i, t * (SIDE // 2), SIDE)
             pairs = [[far_pair(qb, 2 * jj) for jj in range(REMOTE // 2)] for _, _, _, qb in items]
             scores, tops, accs = [], [], []
             for g, (s, half, q, qb) in enumerate(items):
@@ -363,8 +346,10 @@
                     sco = score(q, pairs[g][jj])
                     for part in range(2):
                         piece = sco[:, part * BLK : (part + 1) * BLK]
-                        valid = NEAR + 2 * jj + part < cnt_s[qb]
-                        pieces.append(jnp.where(valid, piece, -1e30))
+                        slot = NEAR + 2 * jj + part
+                        if slot >= LEAST:
+                            piece = jnp.where(slot < cnt_s[qb], piece, -1e30)
+                        pieces.append(piece)
                 scores.append(pieces)
             for g, (s, half, q, qb) in enumerate(items):
                 m = top_v[i, s, half]
@@ -412,7 +397,6 @@
     @pl.loop(1, SEQ)
     def _(d):
         q_copy(1, d).wait_send()
-        kv_copy(0, d).wait_send()
 
     wo_copy.wait()
     for i in range(2):
@@ -450,7 +434,7 @@
     out = pl.pallas_call(
         body,
         out_shape=pltpu.VMEM((OWN, BLK, D), BF16),
-        in_specs=[sm, sm, vm, vm, hbm, hbm],
+        in_specs=[sm, sm, hbm, hbm, hbm, hbm],
         out_specs=vm,
         scratch_shapes=[
             *[pltpu.VMEM((HEADS, OWN, r, 128), BF16) for r in ROWS],
@@ -466,13 +450,15 @@
             pltpu.SMEM((CL, 1, 128), jnp.int32),
             pltpu.VMEM((QB, 128), jnp.int32),
             pltpu.SMEM((QB, 128), jnp.int32),
-            pltpu.VMEM((SIDE, NEAR // 2, BLK, 2 * BLK), F32),
+            pltpu.VMEM((WIDE, NEAR // 2, BLK, 2 * BLK), F32),
             pltpu.VMEM((2, SEQ, 2, BLK, 128), F32),
             pltpu.VMEM((2, SEQ, 2, BLK, 128), F32),
             pltpu.VMEM((2, SEQ, BLK, 128), BF16),
             pltpu.VMEM((2, SEQ, BLK, 128), BF16),
             pltpu.VMEM((2 * BLK, D), BF16),
             pltpu.VMEM((128, 128), F32),
+            pltpu.VMEM((OWN * BLK, D), BF16),
+            pltpu.VMEM((KVB, QB), jnp.int32),
             dma((GROUPS + 1,)),
             dma((CL,)),
             dma((CL,)),
@@ -485,7 +471,7 @@
             dma((2, SEQ)),
             dma((2, SEQ)),
             dma((CH + 4,)),
-            dma((2,)),
+            dma((4,)),
         ],
         compiler_params=pltpu.CompilerParams(
             collective_id=0, has_side_effects=True, vmem_limit_bytes=60 << 20

time: 88.1 us -> 88.5 us (level)
  no operation moved by 1% of the time
where the time goes in v5:
time: 88.5 us; the launch traced here: 87.9 us
  Pallas kernels  87.8 us (99%)
    pallas_call x1, Pallas kernels, on_device(): pl.pallas_call(body, out_shape=pltpu.VMEM((OWN, BLK, D), BF16), in_specs=...  86.8 us

profile of v5, /device:TPU:1, one launch (start us, length us, event | category | flops | bytes accessed | tf_op | source)
XLA Modules:
  0.0 87.9 jit_solution(2986520869671892258)
XLA Ops:
  0.0 86.8 %sublayer.1.x_ref = bf16[4,128,1024]{2,1,0:T(8,128)(2,1)S(1)} custom-call(s32[16,64]{1,0:T(8,128)} %bitcast.2, s32[64]{0:T(128)} %cnt_s.1, bf16[512,1024]{1,0:T(8,128)(2,1)} %nodes_hbm.1, s32[16,64]{1,0:T(8,128)} %bitcast.3, bf16[1024,3072]{1,0:T(8,128)(2,1)} %w_hbm.1, bf16[1024,1024]{1,0:T(8,128)(2,1)} %wo_hbm.1), custom_call_target="tpu_custom_call" | custom-call | tf_op jit(solution)/shard_map/sublayer/pallas_call | solution.py:434
  86.8 1.0 %write_out.1 = bf16[4,128,1024]{2,1,0:T(8,128)(2,1)} custom-call(bf16[4,128,1024]{2,1,0:T(8,128)(2,1)S(1)} %sublayer.1.x_ref), custom_call_target="tpu_custom_call" | custom-call | tf_op jit(solution)/shard_map/write_out/pallas_call | solution.py:481

commit v6 on v5

--- a/solution.py
+++ b/solution.py
@@ -14,7 +14,6 @@
 KVB = 16
 REMOTE = 4
 NEAR = KVB - REMOTE
-LEAST = 13
 QB = 64
 REQ = 16
 CL = 8
@@ -268,27 +267,13 @@
     sm_copy.start()
     sm_copy.wait()
 
-    for c in range(CH):
-        landed(kv_own(c), kv(c))
-        pack(c)
-        if c + 2 < CH:
-            start_after(kv(c + 1), kv_own(c + 2), kv(c + 2))
-        elif c + 2 == CH:
-            start_after(kv(c + 1), q_own(0), qq(0))
-    start_after(qq(0), q_own(1), qq(1))
-
-    def block_of(bufs, b):
-        return [bufs[c][b] for c in range(CH)]
-
-    def pair_of(bufs, b0, b1):
-        return jnp.concatenate(block_of(bufs, b0) + block_of(bufs, b1), axis=0)
-
-    def near_pair(qb, j):
-        return pair_of(kvc, ids_s[j, qb] & (QB - 1), ids_s[j + 1, qb] & (QB - 1))
-
-    def far_pair(qb, j):
-        last = CL * REQ - 1
-        return pair_of(far, far_s[qb, j] & last, far_s[qb, j + 1] & last)
+    def near_keys(qb, jj, chunks):
+        blocks = [ids_s[4 * jj + e, qb] & (QB - 1) for e in range(4)]
+        return jnp.concatenate([kvc[c][b] for b in blocks for c in chunks], axis=0)
+
+    def far_keys(qb, jj, chunks):
+        blocks = [far_s[qb, 4 * jj + e] & (CL * REQ - 1) for e in range(4)]
+        return jnp.concatenate([far[c][b] for b in blocks for c in chunks], axis=0)
 
     def score(q, kv):
         return lax.dot_general(q, kv, (((1,), (1,)), ((), ())), preferred_element_type=F32)
@@ -313,90 +298,107 @@
                 items.append((s, half, q, s * OWN + i + 2 * half))
         return items
 
-    def near(i):
+    def attend(i, begin, count, keys, tiles, chunks):
+        remote, first = keys is far_keys, keys is near_keys and chunks[0] == 0
+        items = items_of(i, begin, count)
+        tops, accs = [None] * count, [None] * count
+        for jj in range(tiles):
+            for g, (s, half, q, qb) in enumerate(items):
+                sco = score(q, keys(qb, jj, chunks))
+                if remote:
+                    lanes = lax.broadcasted_iota(jnp.int32, sco.shape, 1)
+                    sco = jnp.where(lanes < (cnt_s[qb] - NEAR) * (2 * BLK // REMOTE), sco, -1e30)
+                sc[g, jj] = sco
+                top = jnp.maximum(sco[:, :BLK], sco[:, BLK:])
+                tops[g] = top if jj == 0 else jnp.maximum(tops[g], top)
+        for g, (s, half, q, qb) in enumerate(items):
+            top = tops[g] if first else jnp.maximum(tops[g], top_v[i, s, half])
+            tops[g] = jnp.max(top, axis=1, keepdims=True)
+        for jj in range(tiles):
+            for g, (s, half, q, qb) in enumerate(items):
+                a = weigh(sc[g, jj], tops[g], keys(qb, jj, chunks))
+                accs[g] = a if jj == 0 else accs[g] + a
+        for g, (s, half, q, qb) in enumerate(items):
+            if not first:
+                accs[g] = accs[g] + acc_v[i, s, half] * jnp.exp(top_v[i, s, half] - tops[g])
+            if not (remote and chunks[-1] == CH - 1):
+                acc_v[i, s, half] = accs[g]
+                top_v[i, s, half] = jnp.broadcast_to(tops[g], (BLK, 128))
+        return items, accs
+
+    early, late = (0, 1), (2, 3)
+
+    def near(i, chunks):
         @pl.loop(0, 2 * SEQ // WIDE)
         def _(t):
-            items = items_of(i, t * (WIDE // 2), WIDE)
-            tops = [None] * WIDE
-            for jj in range(NEAR // 2):
-                for g, (s, half, q, qb) in enumerate(items):
-                    sco = score(q, near_pair(qb, 2 * jj))
-                    sc[g, jj] = sco
-                    top = jnp.maximum(sco[:, :BLK], sco[:, BLK:])
-                    tops[g] = top if jj == 0 else jnp.maximum(tops[g], top)
-            tops = [jnp.max(top, axis=1, keepdims=True) for top in tops]
-            accs = [None] * WIDE
-            for jj in range(NEAR // 2):
-                for g, (s, half, q, qb) in enumerate(items):
-                    a = weigh(sc[g, jj], tops[g], near_pair(qb, 2 * jj))
-                    accs[g] = a if jj == 0 else accs[g] + a
-            for g, (s, half, q, qb) in enumerate(items):
-                acc_v[i, s, half] = accs[g]
-                top_v[i, s, half] = jnp.broadcast_to(tops[g], (BLK, 128))
-
-    def distant(i):
-        @pl.loop(0, 2 * SEQ // SIDE)
-        def _(t):
-            items = items_of(i, t * (SIDE // 2), SIDE)
-            pairs = [[far_pair(qb, 2 * jj) for jj in range(REMOTE // 2)] for _, _, _, qb in items]
-            scores, tops, accs = [], [], []
-            for g, (s, half, q, qb) in enumerate(items):
-                pieces = []
-                for jj in range(REMOTE // 2):
-                    sco = score(q, pairs[g][jj])
-                    for part in range(2):
-                        piece = sco[:, part * BLK : (part + 1) * BLK]
-                        slot = NEAR + 2 * jj + part
-                        if slot >= LEAST:
-                            piece = jnp.where(slot < cnt_s[qb], piece, -1e30)
-                        pieces.append(piece)
-                scores.append(pieces)
-            for g, (s, half, q, qb) in enumerate(items):
-                m = top_v[i, s, half]
-                for piece in scores[g]:
-                    m = jnp.maximum(m, piece)
-                tops.append(jnp.max(m, axis=1, keepdims=True))
-            for g, (s, half, q, qb) in enumerate(items):
-                acc = acc_v[i, s, half] * jnp.exp(top_v[i, s, half] - tops[g])
-                for jj in range(REMOTE // 2):
-                    both = jnp.concatenate(scores[g][2 * jj : 2 * jj + 2], axis=1)
-                    acc = acc + weigh(both, tops[g], pairs[g][jj])
-                accs.append(acc)
-            low = low_lanes((BLK, 128))
-            for u in range(SIDE // 2):
-                s = items[2 * u][0]
-                left, right = accs[2 * u : 2 * u + 2]
-                lsw, rsw = swap_halves(left), swap_halves(right)
-                value = jnp.where(low, lsw, right)
-                total = jnp.where(low, left, rsw)
-                outs[i, s] = (value / total).astype(BF16)
-
-            for u in range(SIDE // 2):
-                d = t * (SIDE // 2) + u
-
-                @pl.when(d > 0)
-                def _(d=d):
-                    ret_copy(i, lax.rem(me + d, SEQ), d).start()
-
+            attend(i, t * (WIDE // 2), WIDE, near_keys, NEAR // 4, chunks)
+
+    for c in range(2):
+        landed(kv_own(c), kv(c))
+        pack(c)
+        if c == 0:
+            start_after(kv(1), q_own(0), qq(0))
+        else:
+            start_after(qq(0), kv_own(2), kv(2))
     landed(q_own(0), qq(0))
-    near(0)
+    near(0, early)
+    start_after(kv(2), q_own(1), qq(1))
+    landed(kv_own(2), kv(2))
+    pack(2)
+    start_after(qq(1), kv_own(3), kv(3))
     landed(q_own(1), qq(1))
-    near(1)
-
-    for c in range(CH):
-
+    near(1, early)
+    landed(kv_own(3), kv(3))
+    pack(3)
+
+    @pl.loop(0, 2)
+    def _(i):
+        near(i, late)
+
+    far_copy.wait()
+
+    def arrived(c):
         @pl.loop(1, CL)
-        def _(d, c=c):
+        def _(d):
             z_copy(c, d).wait()
 
-    far_copy.wait()
+    arrived(0)
+    arrived(1)
+
+    @pl.loop(0, 4 * SEQ // WIDE)
+    def _(n):
+        i, t = n // (2 * SEQ // WIDE), lax.rem(n, 2 * SEQ // WIDE)
+        attend(i, t * (WIDE // 2), WIDE, far_keys, 1, early)
+
+    arrived(2)
+    arrived(3)
+
+    @pl.loop(0, 4 * SEQ // SIDE)
+    def _(n):
+        i, t = n // (2 * SEQ // SIDE), lax.rem(n, 2 * SEQ // SIDE)
+        items, accs = attend(i, t * (SIDE // 2), SIDE, far_keys, 1, late)
+        low = low_lanes((BLK, 128))
+        for u in range(SIDE // 2):
+            s = items[2 * u][0]
+            left, right = accs[2 * u : 2 * u + 2]
+            lsw, rsw = swap_halves(left), swap_halves(right)
+            value = jnp.where(low, lsw, right)
+            total = jnp.where(low, left, rsw)
+            outs[i, s] = (value / total).astype(BF16)
+
+        for u in range(SIDE // 2):
+            d = t * (SIDE // 2) + u
+
+            @pl.when(d > 0)
+            def _(d=d):
+                ret_copy(i, lax.rem(me + d, SEQ), d).start()
+
     for i in range(2):
-        distant(i)
         ret_own(i).start()
 
     @pl.loop(1, SEQ)
     def _(d):
-        q_copy(1, d).wait_send()
+        kv_copy(3, d).wait_send()
 
     wo_copy.wait()
     for i in range(2):
@@ -450,7 +452,7 @@
             pltpu.SMEM((CL, 1, 128), jnp.int32),
             pltpu.VMEM((QB, 128), jnp.int32),
             pltpu.SMEM((QB, 128), jnp.int32),
-            pltpu.VMEM((WIDE, NEAR // 2, BLK, 2 * BLK), F32),
+            pltpu.VMEM((WIDE, NEAR // 4, BLK, 2 * BLK), F32),
             pltpu.VMEM((2, SEQ, 2, BLK, 128), F32),
             pltpu.VMEM((2, SEQ, 2, BLK, 128), F32),
             pltpu.VMEM((2, SEQ, BLK, 128), BF16),

time: 88.5 us -> 90.1 us (1.018)
  Pallas kernels: 87.8 us -> 89.5 us
    pallas_call x1, Pallas kernels: 86.8 us -> 88.5 us  [on_device(): pl.pallas_call(body, out_shape=pltpu.VMEM((OWN, BLK, D), BF16), in_specs=...]
where the time goes in v6:
time: 90.1 us; the launch traced here: 89.5 us
  Pallas kernels  89.5 us (99%)
    pallas_call x1, Pallas kernels, on_device(): pl.pallas_call(body, out_shape=pltpu.VMEM((OWN, BLK, D), BF16), in_specs=...  88.5 us

profile of v6, /device:TPU:1, one launch (start us, length us, event | category | flops | bytes accessed | tf_op | source)
XLA Modules:
  0.0 89.5 jit_solution(7227311082715239090)
XLA Ops:
  0.0 88.5 %sublayer.1.x_ref = bf16[4,128,1024]{2,1,0:T(8,128)(2,1)S(1)} custom-call(s32[16,64]{1,0:T(8,128)} %bitcast.2, s32[64]{0:T(128)} %cnt_s.1, bf16[512,1024]{1,0:T(8,128)(2,1)} %nodes_hbm.1, s32[16,64]{1,0:T(8,128)} %bitcast.3, bf16[1024,3072]{1,0:T(8,128)(2,1)} %w_hbm.1, bf16[1024,1024]{1,0:T(8,128)(2,1)} %wo_hbm.1), custom_call_target="tpu_custom_call" | custom-call | tf_op jit(solution)/shard_map/sublayer/pallas_call | solution.py:436
  88.5 1.0 %write_out.1 = bf16[4,128,1024]{2,1,0:T(8,128)(2,1)} custom-call(bf16[4,128,1024]{2,1,0:T(8,128)(2,1)S(1)} %sublayer.1.x_ref), custom_call_target="tpu_custom_call" | custom-call | tf_op jit(solution)/shard_map/write_out/pallas_call | solution.py:483

commit v7 on v6

--- a/solution.py
+++ b/solution.py
@@ -267,13 +267,16 @@
     sm_copy.start()
     sm_copy.wait()
 
-    def near_keys(qb, jj, chunks):
-        blocks = [ids_s[4 * jj + e, qb] & (QB - 1) for e in range(4)]
-        return jnp.concatenate([kvc[c][b] for b in blocks for c in chunks], axis=0)
-
-    def far_keys(qb, jj, chunks):
-        blocks = [far_s[qb, 4 * jj + e] & (CL * REQ - 1) for e in range(4)]
-        return jnp.concatenate([far[c][b] for b in blocks for c in chunks], axis=0)
+    def near_keys(qb, pieces):
+        return jnp.concatenate([kvc[c][ids_s[j, qb] & (QB - 1)] for c, j in pieces], axis=0)
+
+    def far_keys(qb, pieces):
+        return jnp.concatenate([far[c][far_s[qb, j] & (CL * REQ - 1)] for c, j in pieces], axis=0)
+
+    def tiles_of(slots, chunks):
+        pieces = [(c, j) for c in chunks for j in range(slots)]
+        per = 2 * BLK // ROWS[0]
+        return [pieces[n : n + per] for n in range(0, len(pieces), per)]
 
     def score(q, kv):
         return lax.dot_general(q, kv, (((1,), (1,)), ((), ())), preferred_element_type=F32)
@@ -298,25 +301,27 @@
                 items.append((s, half, q, s * OWN + i + 2 * half))
         return items
 
-    def attend(i, begin, count, keys, tiles, chunks):
+    def attend(i, begin, count, keys, chunks):
         remote, first = keys is far_keys, keys is near_keys and chunks[0] == 0
         items = items_of(i, begin, count)
+        tiles = tiles_of(REMOTE if remote else NEAR, chunks)
         tops, accs = [None] * count, [None] * count
-        for jj in range(tiles):
+        for jj, tile in enumerate(tiles):
             for g, (s, half, q, qb) in enumerate(items):
-                sco = score(q, keys(qb, jj, chunks))
+                sco = score(q, keys(qb, tile))
                 if remote:
-                    lanes = lax.broadcasted_iota(jnp.int32, sco.shape, 1)
-                    sco = jnp.where(lanes < (cnt_s[qb] - NEAR) * (2 * BLK // REMOTE), sco, -1e30)
-                sc[g, jj] = sco
-                top = jnp.maximum(sco[:, :BLK], sco[:, BLK:])
+                    slot = lax.broadcasted_iota(jnp.int32, sco.shape, 1) // ROWS[0] % REMOTE
+                    sco = jnp.where(slot < cnt_s[qb] - NEAR, sco, -1e30)
+                sc[g, jj, :, : sco.shape[1]] = sco
+                top = sco if sco.shape[1] == BLK else jnp.maximum(sco[:, :BLK], sco[:, BLK:])
                 tops[g] = top if jj == 0 else jnp.maximum(tops[g], top)
         for g, (s, half, q, qb) in enumerate(items):
             top = tops[g] if first else jnp.maximum(tops[g], top_v[i, s, half])
             tops[g] = jnp.max(top, axis=1, keepdims=True)
-        for jj in range(tiles):
+        for jj, tile in enumerate(tiles):
             for g, (s, half, q, qb) in enumerate(items):
-                a = weigh(sc[g, jj], tops[g], keys(qb, jj, chunks))
+                kv = keys(qb, tile)
+                a = weigh(sc[g, jj, :, : kv.shape[0]], tops[g], kv)
                 accs[g] = a if jj == 0 else accs[g] + a
         for g, (s, half, q, qb) in enumerate(items):
             if not first:
@@ -326,26 +331,24 @@
                 top_v[i, s, half] = jnp.broadcast_to(tops[g], (BLK, 128))
         return items, accs
 
-    early, late = (0, 1), (2, 3)
+    early, late = (0, 1, 2), (3,)
 
     def near(i, chunks):
         @pl.loop(0, 2 * SEQ // WIDE)
         def _(t):
-            attend(i, t * (WIDE // 2), WIDE, near_keys, NEAR // 4, chunks)
-
-    for c in range(2):
+            attend(i, t * (WIDE // 2), WIDE, near_keys, chunks)
+
+    for c in early:
         landed(kv_own(c), kv(c))
         pack(c)
         if c == 0:
-            start_after(kv(1), q_own(0), qq(0))
-        else:
-            start_after(qq(0), kv_own(2), kv(2))
+            start_after(kv(1), kv_own(2), kv(2))
+        elif c == 1:
+            start_after(kv(2), q_own(0), qq(0))
+    start_after(qq(0), q_own(1), qq(1))
+    start(kv_own(3), kv(3))
     landed(q_own(0), qq(0))
     near(0, early)
-    start_after(kv(2), q_own(1), qq(1))
-    landed(kv_own(2), kv(2))
-    pack(2)
-    start_after(qq(1), kv_own(3), kv(3))
     landed(q_own(1), qq(1))
     near(1, early)
     landed(kv_own(3), kv(3))
@@ -362,21 +365,20 @@
         def _(d):
             z_copy(c, d).wait()
 
-    arrived(0)
-    arrived(1)
+    for c in early:
+        arrived(c)
 
     @pl.loop(0, 4 * SEQ // WIDE)
     def _(n):
         i, t = n // (2 * SEQ // WIDE), lax.rem(n, 2 * SEQ // WIDE)
-        attend(i, t * (WIDE // 2), WIDE, far_keys, 1, early)
-
-    arrived(2)
+        attend(i, t * (WIDE // 2), WIDE, far_keys, early)
+
     arrived(3)
 
     @pl.loop(0, 4 * SEQ // SIDE)
     def _(n):
         i, t = n // (2 * SEQ // SIDE), lax.rem(n, 2 * SEQ // SIDE)
-        items, accs = attend(i, t * (SIDE // 2), SIDE, far_keys, 1, late)
+        items, accs = attend(i, t * (SIDE // 2), SIDE, far_keys, late)
         low = low_lanes((BLK, 128))
         for u in range(SIDE // 2):
             s = items[2 * u][0]
@@ -398,6 +400,7 @@
 
     @pl.loop(1, SEQ)
     def _(d):
+        q_copy(1, d).wait_send()
         kv_copy(3, d).wait_send()
 
     wo_copy.wait()
@@ -452,7 +455,7 @@
             pltpu.SMEM((CL, 1, 128), jnp.int32),
             pltpu.VMEM((QB, 128), jnp.int32),
             pltpu.SMEM((QB, 128), jnp.int32),
-            pltpu.VMEM((WIDE, NEAR // 4, BLK, 2 * BLK), F32),
+            pltpu.VMEM((WIDE, 5, BLK, 2 * BLK), F32),
             pltpu.VMEM((2, SEQ, 2, BLK, 128), F32),
             pltpu.VMEM((2, SEQ, 2, BLK, 128), F32),
             pltpu.VMEM((2, SEQ, BLK, 128), BF16),

time: 90.1 us -> 89.7 us (level)
  the two profiles are of different devices: /device:TPU:1 before, /device:TPU:28 now
where the time goes in v7:
time: 89.7 us; the launch traced here: 89.5 us
  Pallas kernels  89.4 us (100%)
    pallas_call x1, Pallas kernels, on_device(): pl.pallas_call(body, out_shape=pltpu.VMEM((OWN, BLK, D), BF16), in_specs=...  88.4 us

profile of v7, /device:TPU:28, one launch (start us, length us, event | category | flops | bytes accessed | tf_op | source)
XLA Modules:
  0.0 89.5 jit_solution(7882142019243024042)
XLA Ops:
  0.0 88.4 %sublayer.1.x_ref = bf16[4,128,1024]{2,1,0:T(8,128)(2,1)S(1)} custom-call(s32[16,64]{1,0:T(8,128)} %bitcast.2, s32[64]{0:T(128)} %cnt_s.1, bf16[512,1024]{1,0:T(8,128)(2,1)} %nodes_hbm.1, s32[16,64]{1,0:T(8,128)} %bitcast.3, bf16[1024,3072]{1,0:T(8,128)(2,1)} %w_hbm.1, bf16[1024,1024]{1,0:T(8,128)(2,1)} %wo_hbm.1), custom_call_target="tpu_custom_call" | custom-call | tf_op jit(solution)/shard_map/sublayer/pallas_call | solution.py:439
  88.4 1.0 %write_out.1 = bf16[4,128,1024]{2,1,0:T(8,128)(2,1)} custom-call(bf16[4,128,1024]{2,1,0:T(8,128)(2,1)S(1)} %sublayer.1.x_ref), custom_call_target="tpu_custom_call" | custom-call | tf_op jit(solution)/shard_map/write_out/pallas_call | solution.py:486

commit v8 on v5

--- a/solution.py
+++ b/solution.py
@@ -20,7 +20,7 @@
 CL = 8
 SEQ = 16
 OWN = 4
-ROWS = (32, 32, 32, 32)
+ROWS = (16, 16, 32, 32, 32)
 CH = len(ROWS)
 FIRST = tuple(sum(ROWS[:c]) for c in range(CH))
 GROUPS = 4
@@ -218,6 +218,15 @@
     def group(k):
         return lax.rem(me // GROUPS + k, GROUPS)
 
+    def send_group(c, k):
+        @pl.loop(0, HEADS // GROUPS)
+        def _(h):
+            d = lax.rem(group(k) * (HEADS // GROUPS) + h + SEQ - me, SEQ)
+
+            @pl.when(d > 0)
+            def _():
+                kv_copy(c, d).start()
+
     nodes_copy.wait()
     x0 = jnp.concatenate([nodes[b * BLK : b * BLK + ROWS[0]] for b in range(OWN)], axis=0)
 
@@ -231,16 +240,37 @@
             kvs[0][h0] = kv0.astype(BF16).reshape(OWN, ROWS[0], 128)
             kvs[0][h0 + 1] = t2.astype(BF16).reshape(OWN, ROWS[0], 128)
 
-    pl.semaphore_wait(barrier, SEQ + CL - 2)
-    for d in range(1, CL):
-        list_copy(d).start()
-    for d in range(1, SEQ):
-        kv_copy(0, d).start()
+        @pl.when(k == 0)
+        def _():
+            pl.semaphore_wait(barrier, SEQ + CL - 2)
+
+            @pl.loop(1, CL)
+            def _(d):
+                list_copy(d).start()
+
+        send_group(0, k)
+
     kv_own(0).start()
     wo_copy.start()
 
     @pl.loop(0, GROUPS)
     def _(k):
+        @pl.when(k == GROUPS // 2)
+        def _():
+            @pl.loop(1, CL)
+            def _(d):
+                list_copy(d).wait()
+
+            sm_copy = pltpu.make_async_copy(
+                lrecv.at[pl.ds(1, CL - 1)], lsm.at[pl.ds(1, CL - 1)], sm_sem.at[0]
+            )
+            sm_copy.start()
+            sm_copy.wait()
+
+
+            landed(kv_own(0), kv(0))
+            pack(0)
+
         low = low_lanes((OWN * BLK, 128))
         half = OWN * BLK // 2
         scale = HD**-0.5
@@ -256,19 +286,11 @@
             q1 = jnp.where(low[:half], r1[:half], t1[half:]) * scale
             qs[h0] = q0.astype(BF16).reshape(2, BLK, 128)
             qs[h0 + 1] = q1.astype(BF16).reshape(2, BLK, 128)
-
-    start_after(kv(0), kv_own(1), kv(1))
-    @pl.loop(1, CL)
-    def _(d):
-        list_copy(d).wait()
-
-    sm_copy = pltpu.make_async_copy(
-        lrecv.at[pl.ds(1, CL - 1)], lsm.at[pl.ds(1, CL - 1)], sm_sem.at[0]
-    )
-    sm_copy.start()
-    sm_copy.wait()
-
-    for c in range(CH):
+        send_group(1, k)
+
+    kv_own(1).start()
+    start_after(kv(1), kv_own(2), kv(2))
+    for c in range(1, CH):
         landed(kv_own(c), kv(c))
         pack(c)
         if c + 2 < CH:
@@ -397,6 +419,7 @@
     @pl.loop(1, SEQ)
     def _(d):
         q_copy(1, d).wait_send()
+        kv_copy(0, d).wait_send()
 
     wo_copy.wait()
     for i in range(2):

time: 88.5 us -> 87.5 us (0.989)
  no operation moved by 1% of the time
where the time goes in v8:
time: 87.5 us; the launch traced here: 87.3 us
  Pallas kernels  87.1 us (100%)
    pallas_call x1, Pallas kernels, on_device(): pl.pallas_call(body, out_shape=pltpu.VMEM((OWN, BLK, D), BF16), in_specs=...  86.1 us

profile of v8, /device:TPU:1, one launch (start us, length us, event | category | flops | bytes accessed | tf_op | source)
XLA Modules:
  0.0 87.3 jit_solution(11634916824297461435)
XLA Ops:
  0.0 86.1 %sublayer.1.x_ref = bf16[4,128,1024]{2,1,0:T(8,128)(2,1)S(1)} custom-call(s32[16,64]{1,0:T(8,128)} %bitcast.2, s32[64]{0:T(128)} %cnt_s.1, bf16[512,1024]{1,0:T(8,128)(2,1)} %nodes_hbm.1, s32[16,64]{1,0:T(8,128)} %bitcast.3, bf16[1024,3072]{1,0:T(8,128)(2,1)} %w_hbm.1, bf16[1024,1024]{1,0:T(8,128)(2,1)} %wo_hbm.1), custom_call_target="tpu_custom_call" | custom-call | tf_op jit(solution)/shard_map/sublayer/pallas_call | solution.py:457
  86.1 1.0 %write_out.1 = bf16[4,128,1024]{2,1,0:T(8,128)(2,1)} custom-call(bf16[4,128,1024]{2,1,0:T(8,128)(2,1)S(1)} %sublayer.1.x_ref), custom_call_target="tpu_custom_call" | custom-call | tf_op jit(solution)/shard_map/write_out/pallas_call | solution.py:504

commit v9 on v8

--- a/solution.py
+++ b/solution.py
@@ -20,7 +20,7 @@
 CL = 8
 SEQ = 16
 OWN = 4
-ROWS = (16, 16, 32, 32, 32)
+ROWS = (16, 32, 32, 48)
 CH = len(ROWS)
 FIRST = tuple(sum(ROWS[:c]) for c in range(CH))
 GROUPS = 4

time: 87.5 us -> 87.7 us (level)
  no operation moved by 1% of the time
where the time goes in v9:
time: 87.7 us; the launch traced here: 87.5 us
  Pallas kernels  87.3 us (100%)
    pallas_call x1, Pallas kernels, on_device(): pl.pallas_call(body, out_shape=pltpu.VMEM((OWN, BLK, D), BF16), in_specs=...  86.3 us

profile of v9, /device:TPU:1, one launch (start us, length us, event | category | flops | bytes accessed | tf_op | source)
XLA Modules:
  0.0 87.5 jit_solution(4057948027677435990)
XLA Ops:
  0.0 86.3 %sublayer.1.x_ref = bf16[4,128,1024]{2,1,0:T(8,128)(2,1)S(1)} custom-call(s32[16,64]{1,0:T(8,128)} %bitcast.2, s32[64]{0:T(128)} %cnt_s.1, bf16[512,1024]{1,0:T(8,128)(2,1)} %nodes_hbm.1, s32[16,64]{1,0:T(8,128)} %bitcast.3, bf16[1024,3072]{1,0:T(8,128)(2,1)} %w_hbm.1, bf16[1024,1024]{1,0:T(8,128)(2,1)} %wo_hbm.1), custom_call_target="tpu_custom_call" | custom-call | tf_op jit(solution)/shard_map/sublayer/pallas_call | solution.py:457
  86.3 1.0 %write_out.1 = bf16[4,128,1024]{2,1,0:T(8,128)(2,1)} custom-call(bf16[4,128,1024]{2,1,0:T(8,128)(2,1)S(1)} %sublayer.1.x_ref), custom_call_target="tpu_custom_call" | custom-call | tf_op jit(solution)/shard_map/write_out/pallas_call | solution.py:504
